TPU v7x, 512 devices: a whole 4x8x8 slice. The times are simulated.
512 devices in a mesh: grp: 16 (over z_lo, x), sp: 32 (over z_hi, y, core).
Axes of the slice: x: 4, y: 8, z: 8 (z_hi: 2, z_lo: 4; z = z_hi * 4 + z_lo), core: 2. Of those that a mesh axis runs over, the one named last changes fastest.
Arguments:
- qkv: bfloat16 [16384, 3, 4096], P(('grp', 'sp')), may hold values from -128 to 128
- kv_cache: bfloat16 [32, 2, 3, 512, 4096], P('grp', None, None, None, 'sp'), may hold values from -6 to 6
- cycle_slot: int32 [32], P('grp'), may hold values from 0 to 2, as said below
- valid_count: int32 [32], P('grp'), may hold values from 0 to 3
- span_pos: int32 [32], P('grp'), may hold values from 0 to 63
- dec_in: bfloat16 [32, 3, 32, 32, 384], P('grp', None, 'sp'), may hold values from -6 to 6
- dec_cache: bfloat16 [32, 2, 32, 32, 384], P('sp', None, None, 'grp'), may hold values from -6 to 6
- time_weight: bfloat16 [3, 384, 768], replicated, may hold values from -0.1875 to 0.1875
- time_bias: float32 [768], replicated, may hold values from -3 to 3
Outputs:
- attention: bfloat16 [16384, 4096], P(('grp', 'sp'))
- decoded: bfloat16 [32, 6, 32, 32, 384], P('sp', None, None, 'grp')
Inputs may be any that keep to these rules, and one draw needn't show every extreme that they name: Where valid_count is under 3, cycle_slot equals it.
All inputs are finite; a program needn't handle non-finite values.
Results may differ from a plain program's by a relative error of at most 0.03.
The roundings to bfloat16 on the way count: a program that leaves them out, or rounds other values in their place, can miss the bound.
Values may be sent and summed in bfloat16 or wider, within the bound.
A program may use at most 64 MiB of HBM per device.

v0:
```python
import math

import jax
import jax.numpy as jnp
from jax import lax
from jax.sharding import PartitionSpec as P

HS = 128
CYCLE = 3


def rotate_rows(values_in, positions):
    half_dim = values_in.shape[-1] // 2
    frequency = jnp.exp(-math.log(10000.0) * jnp.arange(half_dim, dtype=jnp.float32) / half_dim)
    angles = positions[:, :, None] * frequency[None, None, :]
    cosine = jnp.cos(angles)[:, :, None, :]
    sine_part = jnp.sin(angles)[:, :, None, :]
    first_half = values_in[..., :half_dim]
    second_half = values_in[..., half_dim:]
    return jnp.concatenate(
        [
            first_half * cosine - second_half * sine_part,
            first_half * sine_part + second_half * cosine,
        ],
        -1,
    )


def upsample_frames(latent, cached, time_weight, time_bias):
    shape_in = latent.shape
    frame_count = shape_in[1]
    channels = shape_in[-1]
    frames_all = jnp.concatenate([cached, latent], 1)
    conv_out = jnp.dot(
        frames_all[:, 0:frame_count].reshape(-1, channels),
        time_weight[0],
        preferred_element_type=jnp.float32,
    )
    for offset in range(1, 3):
        conv_out = conv_out + jnp.dot(
            frames_all[:, offset : offset + frame_count].reshape(-1, channels),
            time_weight[offset],
            preferred_element_type=jnp.float32,
        )
    conv_out = conv_out + time_bias[None, :]
    conv_out = conv_out.reshape(shape_in[0], frame_count, shape_in[2], shape_in[3], 2, channels)
    conv_out = jnp.moveaxis(conv_out, 4, 2)
    return conv_out.reshape(
        shape_in[0], 2 * frame_count, shape_in[2], shape_in[3], channels
    ).astype(jnp.bfloat16)


def on_device(
    qkv, kv_cache, cycle_slot, valid_count, span_pos, dec_in, dec_cache, time_weight, time_bias
):
    pieces = lax.all_to_all(qkv, "sp", split_axis=2, concat_axis=0, tiled=True)
    videos_here = cycle_slot.shape[0]
    video_len = pieces.shape[0] // videos_here
    local_heads = pieces.shape[2] // HS
    tokens_block = pieces.reshape(videos_here, video_len, 3, local_heads, HS)
    cache_pair = kv_cache.reshape(videos_here, 2, CYCLE * video_len, local_heads, HS)
    positions = (
        span_pos[:, None] * video_len + jnp.arange(video_len, dtype=jnp.int32)[None, :]
    ).astype(jnp.float32)
    queries = rotate_rows(tokens_block[:, :, 0].astype(jnp.float32), positions).astype(jnp.bfloat16)
    key_now = rotate_rows(tokens_block[:, :, 1].astype(jnp.float32), positions).astype(jnp.bfloat16)
    key_rows = jnp.concatenate([cache_pair[:, 0], key_now], 1)
    value_rows = jnp.concatenate([cache_pair[:, 1], tokens_block[:, :, 2]], 1)
    scores = jnp.einsum(
        "vthd,vshd->vhts", queries, key_rows, preferred_element_type=jnp.float32
    ) / math.sqrt(HS)
    slot_index = jnp.arange((CYCLE + 1) * video_len, dtype=jnp.int32) // video_len
    valid_keys = (slot_index[None, :] == CYCLE) | (slot_index[None, :] < valid_count[:, None]) & (
        slot_index[None, :] != cycle_slot[:, None]
    )
    scores = jnp.where(valid_keys[:, None, None, :], scores, -jnp.inf)
    row_max = jnp.max(scores, -1, keepdims=True)
    weights = jnp.exp(scores - row_max)
    weight_sum = jnp.sum(weights, -1)
    rounded = weights.astype(jnp.bfloat16)
    mixed_out = jnp.einsum(
        "vhts,vshd->vthd", rounded, value_rows, preferred_element_type=jnp.float32
    )
    mixed_out = mixed_out / jnp.moveaxis(weight_sum, 1, 2)[..., None]
    mixed_out = mixed_out.astype(jnp.bfloat16).reshape(videos_here * video_len, local_heads * HS)
    attention = lax.all_to_all(mixed_out, "sp", split_axis=0, concat_axis=1, tiled=True)
    cached_here = lax.all_to_all(
        lax.all_to_all(dec_cache, "sp", split_axis=2, concat_axis=0, tiled=True),
        "grp",
        split_axis=0,
        concat_axis=3,
        tiled=True,
    )
    upsampled = upsample_frames(dec_in, cached_here, time_weight, time_bias)
    decoded = lax.all_to_all(
        lax.all_to_all(upsampled, "grp", split_axis=3, concat_axis=0, tiled=True),
        "sp",
        split_axis=0,
        concat_axis=2,
        tiled=True,
    )
    return (attention, decoded)


def solution(mesh):
    placed = (
        P(("grp", "sp"), None, None),
        P("grp", None, None, None, "sp"),
        P("grp"),
        P("grp"),
        P("grp"),
        P("grp", None, "sp", None, None),
        P("sp", None, None, "grp", None),
        P(),
        P(),
    )
    return jax.shard_map(
        on_device,
        mesh=mesh,
        in_specs=placed,
        out_specs=(P(("grp", "sp"), None), P("sp", None, None, "grp", None)),
        check_vma=False,
    )
```

profile of v0, /device:TPU:1, one launch (start us, length us, event | category | flops | bytes accessed | tf_op | source)
XLA Modules:
  0.0 153.4 jit_solution(8614771477382792548)
XLA Ops:
  0.6 0.0 copy-start.4
  0.6 0.0 copy-start.5
  0.7 1.0 copy.53
  1.7 29.3 %all_to_all.106 = bf16[1,2,32,2,384]{4,3,1,0,2:T(2,128)(2,1)S(1)} all-to-all(bf16[1,2,32,2,384]{4,3,1,0,2:T(2,128)(2,1)S(1)} %copy.53), channel_id=1, replica_groups=mesh['grp'=16,'sp'=32] {'sp'}, dimensions={2} | all-to-all | bytes 196608 | tf_op jit(solution)/shard_map/all_to_all | solution.py:88
  30.9 14.3 %all_to_all.107 = bf16[32,2,1,2,384]{4,3,1,2,0:T(2,128)(2,1)S(1)} all-to-all(bf16[32,2,1,2,384]{4,3,1,2,0:T(2,128)(2,1)S(1)} %bitcast.109), channel_id=1, replica_groups=mesh['grp'=16,'sp'=32] {'grp'}, dimensions={0} | all-to-all | bytes 196608 | tf_op jit(solution)/shard_map/all_to_all | solution.py:87
  45.2 0.1 copy.55
  45.3 0.0 copy-start.1
  45.3 1.0 constant_dynamic-update-slice_fusion
  46.4 1.4 fusion.37
  47.7 1.4 convolution_add_fusion.1
  49.1 0.0 copy-done.4
  49.1 0.0 copy-done.5
  49.1 1.4 fusion.10
  50.5 0.1 convert_element_type.87
  50.7 1.0 copy.57
  51.7 3.5 %all-to-all-start.4 = ((bf16[2,6,1,32,384]{4,0,2,1,3:T(2,128)(2,1)}), bf16[2,6,1,32,384]{4,0,2,1,3:T(2,128)(2,1)S(1)}, u32[]{:S(2)}, u32[]{:S(2)}) async-start(bf16[2,6,1,32,384]{4,0,2,1,3:T(2,128)(2,1)} %copy.57), calls=%async_computation.4 | async-start | bytes 589824 | tf_op jit(solution)/shard_map/all_to_all | solution.py:96
  55.2 0.0 copy-done.1
  55.2 0.0 copy-start
  55.2 4.6 %copy.48 = bf16[32,3,4096]{0,1,2:T(4,128)(2,1)} copy(bf16[32,3,4096]{2,0,1:T(8,128)(2,1)S(1)} %copy-done.1) | data formatting | bytes 1572864 | tf_op args[0]
  59.9 7.2 %reshape.261 = bf16[32,2,6144]{2,1,0:T(2,128)(2,1)} reshape(bf16[4096,3,32]{2,1,0:T(4,128)(2,1)} %bitcast.100) | data formatting | bytes 1572864
  67.1 0.0 copy-done
  67.1 0.1 copy.47
  67.2 0.0 all-to-all-done.4
  67.2 6.5 %all-to-all-start = ((bf16[32,2,6144]{2,1,0:T(2,128)(2,1)}), bf16[32,2,6144]{2,1,0:T(2,128)(2,1)S(1)}, u32[]{:S(2)}, u32[]{:S(2)}) async-start(bf16[32,2,6144]{2,1,0:T(2,128)(2,1)} %reshape.261), calls=%async_computation | async-start | bytes 1572864 | tf_op jit(solution)/shard_map/all_to_all | solution.py:56
  73.8 0.0 copy-done.8
  73.8 0.1 add_convert_fusion
  73.9 0.0 copy-done.6
  73.9 0.0 copy-done.7
  73.9 0.1 and_or_fusion
  74.0 1.3 slice_bitcast_fusion.1
  75.3 0.2 copy.58
  75.5 0.9 copy.59
  76.4 22.7 %all-to-all-done = bf16[32,2,6144]{2,1,0:T(2,128)(2,1)S(1)} async-done(((bf16[32,2,6144]{2,1,0:T(2,128)(2,1)}), bf16[32,2,6144]{2,1,0:T(2,128)(2,1)S(1)}, u32[]{:S(2)}, u32[]{:S(2)}) %all-to-all-start) | async-done | bytes 786464 | tf_op jit(solution)/shard_map/all_to_all | solution.py:56
  99.1 5.7 %all-to-all-start.5 = ((bf16[32,6,1,2,384]{4,3,1,2,0:T(2,128)(2,1)}), bf16[32,6,1,2,384]{4,3,1,2,0:T(2,128)(2,1)S(1)}, u32[]{:S(2)}, u32[]{:S(2)}) async-start(bf16[32,6,1,2,384]{4,3,1,2,0:T(2,128)(2,1)} %bitcast.37), calls=%async_computation.5 | async-start | bytes 589824 | tf_op jit(solution)/shard_map/all_to_all | solution.py:95
  104.8 4.9 %reshape.262 = bf16[4096,3,32]{2,1,0:T(4,128)(2,1)} reshape(bf16[32,2,6144]{2,1,0:T(2,128)(2,1)S(1)} %all-to-all-done) | data formatting | bytes 1572864
  109.8 5.5 %copy.49 = bf16[32,3,32,128]{3,0,2,1:T(8,128)(2,1)S(1)} copy(bf16[32,3,32,128]{0,1,3,2:T(4,128)(2,1)} %bitcast.99) | data formatting | bytes 1572864 | tf_op jit(solution)/shard_map/all_to_all | solution.py:56
  115.3 0.1 slice_bitcast_fusion.4
  115.4 2.5 %fusion.56 = (bf16[2,512,64]{2,1,0:T(8,128)(2,1)S(1)}, bf16[2,512,64]{2,1,0:T(8,128)(2,1)S(1)}, bf16[2,512,1,64]{3,1,0,2:T(8,128)(2,1)S(1)}, bf16[2,512,1,64]{3,1,0,2:T(8,128)(2,1)S(1)}) fusion(f32[2,512,1,128]{3,1,0,2:T(8,128)S(1)} %get-tuple-element.12, f32[64]{0:T(128)S(1)} %multiply_exponential_fusion, f32[2,512]{1,0:T(2,128)S(1)} %add_convert_fusion, ...), kind=kLoop, calls=%fused_computation.61 | loop fusion | flops 1114112 | bytes 1577216 | tf_op jit(solution)/shard_map/concatenate | solution.py:20
  117.9 0.0 copy-done.3
  117.9 1.9 %fusion = (f32[2,512]{1,0:T(2,128)S(1)}, f32[2,512,2048]{2,1,0:T(8,128)S(1)}) fusion(pred[2,2048]{1,0:T(4,128)(4,1)S(1)} %and_or_fusion, bf16[2,512,1,64]{3,1,0,2:T(8,128)(2,1)S(1)} %get-tuple-element.19, bf16[2,512,1,64]{3,1,0,2:T(8,128)(2,1)S(1)} %get-tuple-element.20, bf16[2,1536,1,128]{3,1,0,2:T(8,128)(2,1)S(1)} %copy-done.3, ...), kind=kOutput, calls=%fused_computation.2 | convolution fusion | flops 546831360 | bytes 9707520 | tf_op jit(solution)/shard_map/vthd,vshd->vhts/dot_general | solution.py:69
  119.8 1.9 %fusion.1 = f32[2,512]{1,0:T(2,128)S(1)} fusion(f32[2,512,2048]{2,1,0:T(8,128)S(1)} %get-tuple-element.22, f32[2,512]{1,0:T(2,128)S(1)} %get-tuple-element.21, pred[2,2048]{1,0:T(4,128)(4,1)S(1)} %and_or_fusion), kind=kLoop, calls=%fused_computation.3 | loop fusion | flops 8387584 | bytes 8400896 | tf_op jit(solution)/shard_map/reduce_sum | solution.py:79
  121.7 2.3 %fusion.24 = bf16[2,512,1,128]{1,3,0,2:T(8,128)(2,1)S(1)} fusion(f32[2,512,2048]{2,1,0:T(8,128)S(1)} %get-tuple-element.22, f32[2,512]{1,0:T(2,128)S(1)} %get-tuple-element.21, pred[2,2048]{1,0:T(4,128)(4,1)S(1)} %and_or_fusion, bf16[2,512,1,128]{3,1,0,2:T(8,128)(2,1)S(1)} %get-tuple-element.10, bf16[2,1536,1,128]{3,1,0,2:T(8,128)(2,1)S(1)} %copy-done.2, ...), kind=kOutput, calls=%fused_computation.23 | convolution fusion | flops 547618816 | bytes 9711616 | tf_op jit(solution)/shard_map/vhts,vshd->vthd/dot_general | solution.py:81
  124.0 0.8 copy.51
  124.9 0.0 all-to-all-done.5
  124.9 12.3 %all-to-all-start.1 = ((bf16[32,32,128]{2,1,0:T(8,128)(2,1)}), bf16[32,32,128]{2,1,0:T(8,128)(2,1)S(1)}, u32[]{:S(2)}, u32[]{:S(2)}) async-start(bf16[32,32,128]{2,1,0:T(8,128)(2,1)} %bitcast.18), calls=%async_computation.1 | async-start | bytes 524288 | tf_op jit(solution)/shard_map/all_to_all | solution.py:86
  137.2 0.9 copy.61
  138.1 14.5 %all-to-all-done.1 = bf16[32,32,128]{2,1,0:T(8,128)(2,1)S(1)} async-done(((bf16[32,32,128]{2,1,0:T(8,128)(2,1)}), bf16[32,32,128]{2,1,0:T(8,128)(2,1)S(1)}, u32[]{:S(2)}, u32[]{:S(2)}) %all-to-all-start.1) | async-done | bytes 262176 | tf_op jit(solution)/shard_map/all_to_all | solution.py:86
  152.7 0.7 copy_bitcast_fusion
  (14 shorter events, 0.2 us)
Async XLA Ops:
  0.6 48.5 %copy-start.4 = (bf16[2,3,1,32,384]{4,3,2,1,0:T(8,128)(2,1)S(1)}, bf16[2,3,1,32,384]{4,3,2,1,0:T(8,128)(2,1)}, u32[]{:S(2)}) copy-start(bf16[2,3,1,32,384]{4,3,2,1,0:T(8,128)(2,1)} %param.14) | copy-start | bytes 442372
  0.6 48.5 %copy-start.5 = (f32[768]{0:T(1024)S(1)}, f32[768]{0:T(1024)}, u32[]{:S(2)}) copy-start(f32[768]{0:T(1024)} %param.17) | copy-start | bytes 9220
  45.3 9.9 %copy-start.1 = (bf16[32,3,4096]{2,0,1:T(8,128)(2,1)S(1)}, bf16[32,3,4096]{2,0,1:T(8,128)(2,1)}, u32[]{:S(2)}) copy-start(bf16[32,3,4096]{2,0,1:T(8,128)(2,1)} %param.9) | copy-start | bytes 2359300
  51.7 15.6 %all-to-all-start.4 = ((bf16[2,6,1,32,384]{4,0,2,1,3:T(2,128)(2,1)}), bf16[2,6,1,32,384]{4,0,2,1,3:T(2,128)(2,1)S(1)}, u32[]{:S(2)}, u32[]{:S(2)}) async-start(bf16[2,6,1,32,384]{4,0,2,1,3:T(2,128)(2,1)} %copy.57), calls=%async_computation.4 | async-start | bytes 589824 | tf_op jit(solution)/shard_map/all_to_all | solution.py:96
  55.2 11.9 %copy-start = (bf16[2,2,3,512,128]{4,3,2,1,0:T(8,128)(2,1)S(1)}, bf16[2,2,3,512,128]{4,3,2,1,0:T(8,128)(2,1)}, u32[]{:S(2)}) copy-start(bf16[2,2,3,512,128]{4,3,2,1,0:T(8,128)(2,1)} %param.10) | copy-start | bytes 4718596
  59.9 13.9 %copy-start.8 = (s32[2]{0:T(128)S(1)}, s32[2]{0:T(128)}, u32[]{:S(2)}) copy-start(s32[2]{0:T(128)} %param.13) | copy-start | bytes 28
  59.9 14.0 %copy-start.6 = (s32[2]{0:T(128)S(1)}, s32[2]{0:T(128)}, u32[]{:S(2)}) copy-start(s32[2]{0:T(128)} %param.11) | copy-start | bytes 28
  59.9 14.0 %copy-start.7 = (s32[2]{0:T(128)S(1)}, s32[2]{0:T(128)}, u32[]{:S(2)}) copy-start(s32[2]{0:T(128)} %param.12) | copy-start | bytes 28
  67.2 31.9 %all-to-all-start = ((bf16[32,2,6144]{2,1,0:T(2,128)(2,1)}), bf16[32,2,6144]{2,1,0:T(2,128)(2,1)S(1)}, u32[]{:S(2)}, u32[]{:S(2)}) async-start(bf16[32,2,6144]{2,1,0:T(2,128)(2,1)} %reshape.261), calls=%async_computation | async-start | bytes 1572864 | tf_op jit(solution)/shard_map/all_to_all | solution.py:56
  99.1 25.7 %all-to-all-start.5 = ((bf16[32,6,1,2,384]{4,3,1,2,0:T(2,128)(2,1)}), bf16[32,6,1,2,384]{4,3,1,2,0:T(2,128)(2,1)S(1)}, u32[]{:S(2)}, u32[]{:S(2)}) async-start(bf16[32,6,1,2,384]{4,3,1,2,0:T(2,128)(2,1)} %bitcast.37), calls=%async_computation.5 | async-start | bytes 589824 | tf_op jit(solution)/shard_map/all_to_all | solution.py:95
  109.8 8.1 %copy-start.3 = (bf16[2,1536,1,128]{3,1,0,2:T(8,128)(2,1)S(1)}, bf16[2,1536,1,128]{3,1,0,2:T(8,128)(2,1)}, u32[]{:S(2)}) copy-start(bf16[2,1536,1,128]{3,1,0,2:T(8,128)(2,1)} %get-tuple-element.9) | copy-start | bytes 2359300
  119.8 1.9 %copy-start.2 = (bf16[2,1536,1,128]{3,1,0,2:T(8,128)(2,1)S(1)}, bf16[2,1536,1,128]{3,1,0,2:T(8,128)(2,1)}, u32[]{:S(2)}) copy-start(bf16[2,1536,1,128]{3,1,0,2:T(8,128)(2,1)} %get-tuple-element.8) | copy-start | bytes 2359300
  124.9 27.8 %all-to-all-start.1 = ((bf16[32,32,128]{2,1,0:T(8,128)(2,1)}), bf16[32,32,128]{2,1,0:T(8,128)(2,1)S(1)}, u32[]{:S(2)}, u32[]{:S(2)}) async-start(bf16[32,32,128]{2,1,0:T(8,128)(2,1)} %bitcast.18), calls=%async_computation.1 | async-start | bytes 524288 | tf_op jit(solution)/shard_map/all_to_all | solution.py:86
where the time goes:
time: 155 us; the launch traced here: 153 us
  blocking collectives  43.5 us (28%)
  waiting for transfers between devices  37.2 us (24%)
  local copies, waits for them, and re-layouts  30.6 us (20%)
  starting transfers between devices  28.1 us (18%)
  matrix products  8.34 us (5%)
  other arithmetic  4.66 us (3%)
    all_to_all x1, blocking collectives, on_device(): lax.all_to_all(dec_cache, 'sp', split_axis=2, concat_axis=0, tiled=True)  29.3 us
    all_to_all x1, waiting for transfers between devices, on_device(): pieces = lax.all_to_all(qkv, 'sp', split_axis=2, concat_axis=0, tiled=True)  22.7 us
    unnamed x25, local copies, waits for them, and re-layouts  18.8 us
    all_to_all x1, waiting for transfers between devices, on_device(): lax.all_to_all(mixed_out, 'sp', split_axis=0, concat_axis=1, tiled=True)  14.5 us
    all_to_all x1, blocking collectives, on_device(): lax.all_to_all(lax.all_to_all(dec_cache, 'sp', split_axis=2, concat_axis=...  14.3 us
    all_to_all x1, starting transfers between devices, on_device(): lax.all_to_all(mixed_out, 'sp', split_axis=0, concat_axis=1, tiled=True)  12.3 us
    all_to_all x1, starting transfers between devices, on_device(): pieces = lax.all_to_all(qkv, 'sp', split_axis=2, concat_axis=0, tiled=True)  6.53 us
    all_to_all x1, starting transfers between devices, on_device(): lax.all_to_all(lax.all_to_all(upsampled, 'grp', split_axis=3, concat_axis...  5.72 us
  transfers between devices with their start and end apart: 4, of which 2 were waited for; matrix products, arithmetic and copies ran while one was open for 23% of the time, Pallas kernels for 0%

commit v1 on v0

v1 whole, which is shorter than its diff:
```python
import math

import jax
import jax.numpy as jnp
import numpy as np
from jax import lax
from jax.experimental import pallas as pl
from jax.experimental.pallas import tpu as pltpu
from jax.sharding import PartitionSpec as P

HS = 128
CYCLE = 3
MESH = pl.DeviceIdType.MESH
NEG = -1e30
C2 = math.log2(math.e) / math.sqrt(HS)
HALF = 16
TOK = 32
VT = 512
FR = 3
CH = 384
LT = CH // 128


def rope_tables():
    f = np.exp(-math.log(10000.0) * np.arange(64, dtype=np.float64) / 64)
    ang = np.arange(VT, dtype=np.float64)[:, None] * np.concatenate([f, f])[None, :]
    sign = np.concatenate([-np.ones(64), np.ones(64)])
    return np.cos(ang).astype(np.float32), (np.sin(ang) * sign).astype(np.float32)


def dot_t(a, b):
    return lax.dot_general(a, b, (((1,), (1,)), ((), ())), preferred_element_type=jnp.float32)


def dot(a, b):
    return lax.dot_general(a, b, (((1,), (0,)), ((), ())), preferred_element_type=jnp.float32)


def attend(q, parts):
    scores = [dot_t(q, k) if bias is None else dot_t(q, k) + bias for k, _, bias in parts]
    top = jnp.max(scores[0], axis=1, keepdims=True)
    for s in scores[1:]:
        top = jnp.maximum(top, jnp.max(s, axis=1, keepdims=True))
    top = top * C2
    total, acc = None, None
    for s, (_, v, _) in zip(scores, parts):
        w = jnp.exp2(s * C2 - top)
        t = jnp.sum(w, axis=1, keepdims=True)
        o = dot(w.astype(jnp.bfloat16), v)
        total = t if total is None else total + t
        acc = o if acc is None else acc + o
    return top, total, acc


def kernel(
    slot_ref, count_ref, base_ref, qkv, cache_hbm, dec_in, dec_cache, weight_hbm, bias_ref, cos_hbm, sin_hbm,
    out, decoded,
    rx, fq, oc, oc_out, lse_in, lse_out, ob, cache, weight, tabs, cosv, sinv, kself, sendd, frames, outd,
    s_send, s_fwd, s_oc, s_o, s_dec, r_qb, r_a, r_b, r_fq, r_oc, r_lse, r_o, r_dec, l_own, l_cache, l_w, l_tab, l_dc, l_ds, l_out,
):
    g = lax.axis_index("grp")
    s = lax.axis_index("sp")
    half = s // HALF
    me = s % HALF
    y = me // 2
    c = me % 2
    partner = (s + HALF) % 32
    other = 1 - half

    def peer(k, cc):
        step = (k // 2 + 1) * (1 - 2 * (k % 2))
        return ((y + step + 8) % 8) * 2 + (c + cc) % 2

    def for_peers(fn):
        def body(i, _):
            fn(peer(i // 2, i % 2))
            return 0
        lax.fori_loop(0, 14, body, 0)
        fn(y * 2 + (1 - c))

    bar = pltpu.get_barrier_semaphore()
    for_peers(lambda t: pl.semaphore_signal(bar, 1, device_id=(g, half * HALF + t), device_id_type=MESH))
    pl.semaphore_signal(bar, 1, device_id=(g, partner), device_id_type=MESH)
    src_g = s // 2
    mine = (src_g == g).astype(jnp.int32)

    def greet(i, _):
        pl.semaphore_signal(bar, 1, device_id=(src_g, (s + 1 + i) % 32), device_id_type=MESH)
        return 0
    lax.fori_loop(0, 31, greet, 0)

    @pl.when(src_g != g)
    def _():
        pl.semaphore_signal(bar, 1, device_id=(src_g, s), device_id_type=MESH)

    def cols(h):
        return pl.ds(pl.multiple_of(h * HS, HS), HS)

    head = (s, partner)
    own = [pltpu.make_async_copy(qkv.at[:, :, cols(head[j])], rx.at[j, :, me], l_own.at[j]) for j in range(2)]
    for cp in own:
        cp.start()
    c_tab = [pltpu.make_async_copy(h, tabs.at[i], l_tab.at[i]) for i, h in enumerate((cos_hbm, sin_hbm))]
    for cp in c_tab:
        cp.start()
    c_ds = pltpu.make_async_copy
    ds_copies = []
    for v in range(2):
        for j in range(LT):
            cp = pltpu.make_async_copy(dec_in.at[v, :, 0, :, pl.ds(j * 128, 128)], sendd.reshape(2, FR, LT, 32, 128).at[v, :, j], l_ds.at[v * LT + j])
            cp.start()
            ds_copies.append(cp)
    c_cache = pltpu.make_async_copy(cache_hbm, cache, l_cache)
    c_cache.start()
    dc_copies = []
    for j in range(LT):
        cp = pltpu.make_async_copy(dec_cache.at[0, :, :, :, pl.ds(j * 128, 128)], frames.at[pl.ds(0, 2), j], l_dc.at[j])
        cp.start()
        dc_copies.append(cp)
    c_w = pltpu.make_async_copy(weight_hbm, weight, l_w)
    c_w.start()

    pl.semaphore_wait(bar, 15 + 1 + 32 - mine)

    def send(part, n, j, t, rsem):
        pltpu.make_async_remote_copy(
            qkv.at[pl.ds(part, n), :, cols(half * HALF + t if j == 0 else other * HALF + t)],
            rx.at[j, pl.ds(part, n), me], s_send, rsem,
            device_id=(g, half * HALF + t), device_id_type=MESH,
        ).start()

    for_peers(lambda t: send(0, 1, 1, t, r_qb.at[me]))
    for_peers(lambda t: send(0, 3, 0, t, r_a))
    for cp in ds_copies:
        cp.wait()

    def send_frames(gd, v):
        return pltpu.make_async_remote_copy(
            sendd.at[v, :, :, gd], frames.at[pl.ds(2, FR), :, s], s_dec, r_dec,
            device_id=(gd, 2 * g + v), device_id_type=MESH,
        )

    def send_far(i, _):
        send_frames((g + 1 + i // 2) % 16, i % 2).start()
        return 0
    lax.fori_loop(0, 30, send_far, 0)
    for v in range(2):
        @pl.when(s != 2 * g + v)
        def _():
            send_frames(g, v).start()

        @pl.when(s == 2 * g + v)
        def _():
            pltpu.make_async_copy(sendd.at[v, :, :, g], frames.at[pl.ds(2, FR), :, s], r_dec).start()
    for_peers(lambda t: send(1, 2, 1, t, r_b))

    for cp in c_tab:
        cp.wait()

    def make_tables(i, _):
        rows = pl.ds(pl.multiple_of(i * 128, 128), 128)
        ct, st = tabs[0, rows, :], tabs[1, rows, :]
        for v in range(2):
            cb, sb = base_ref[pl.ds(v, 1), :], base_ref[pl.ds(2 + v, 1), :]
            cosv[v, rows, :] = ct * cb - st * sb
            sinv[v, rows, :] = st * cb + ct * sb
        return 0
    lax.fori_loop(0, 4, make_tables, 0)

    def rotate(x, v, row, n):
        x = x.astype(jnp.float32)
        rows = pl.ds(pl.multiple_of(row, n), n)
        return (x * cosv[v, rows, :] + pltpu.roll(x, 64, 1) * sinv[v, rows, :]).astype(jnp.bfloat16)

    def forward(t):
        pltpu.make_async_remote_copy(
            rx.at[1, 0, t], fq.at[t], s_fwd, r_fq.at[t // 4],
            device_id=(g, partner), device_id_type=MESH,
        ).start()

    for cp in own:
        cp.wait()
    forward(me)

    def wait_forward(t):
        pltpu.make_async_copy(rx.at[1, 0, t], rx.at[1, 0, t], r_qb.at[t]).wait()
        forward(t)
    for_peers(wait_forward)

    eye = lax.broadcasted_iota(jnp.int32, (128, 128), 0) == lax.broadcasted_iota(jnp.int32, (128, 128), 1)

    def slots(v):
        cs, vc = slot_ref[v], count_ref[v]
        s0 = jnp.where(cs == 0, 1, 0)
        s1 = jnp.where(cs == 2, 1, 2)
        return [(sl, jnp.where(sl < vc, 0.0, NEG)) for sl in (s0, s1)]

    c_cache.wait()
    there = slots(other)

    def cross(i, _):
        pltpu.make_async_copy(fq.at[pl.ds(i * 4, 4)], fq.at[pl.ds(i * 4, 4)], r_fq.at[i]).wait()
        q = rotate(fq[pl.ds(i * 4, 4)].reshape(128, HS), other, i * 128, 128)
        top, total, acc = attend(q, [(cache[other, 0, sl], cache[other, 1, sl], b) for sl, b in there])
        oc_out[i] = (acc / total).astype(jnp.bfloat16)
        lse = jnp.broadcast_to(top + jnp.log2(total), (128, 128))
        lse_out[i] = jnp.broadcast_to(jnp.sum(jnp.where(eye, lse, 0.0), axis=0, keepdims=True), (8, 128))
        pltpu.make_async_remote_copy(oc_out.at[i], oc.at[i], s_oc.at[0], r_oc.at[i], device_id=(g, partner), device_id_type=MESH).start()
        pltpu.make_async_remote_copy(lse_out.at[i], lse_in.at[i], s_oc.at[1], r_lse.at[i], device_id=(g, partner), device_id_type=MESH).start()
        return 0
    lax.fori_loop(0, 4, cross, 0)

    def send_out(j, t):
        pltpu.make_async_remote_copy(
            ob.at[j, t], out.at[:, cols(head[j])], s_o, r_o,
            device_id=(g, half * HALF + t), device_id_type=MESH,
        ).start()

    def own_out(j):
        return pltpu.make_async_copy(ob.at[j, me], out.at[:, cols(head[j])], l_own.at[j])

    def rotate_keys(j):
        def body(i, _):
            kself[pl.ds(pl.multiple_of(i * 128, 128), 128), :] = rotate(rx[j, 1, pl.ds(i * 4, 4)].reshape(128, HS), half, i * 128, 128)
            return 0
        lax.fori_loop(0, 4, body, 0)

    pltpu.make_async_copy(rx.at[0, :, pl.ds(0, 15)], rx.at[0, :, pl.ds(0, 15)], r_a).wait()
    here = slots(half)
    rotate_keys(0)

    def whole(i, _):
        q = rotate(rx[0, 0, pl.ds(i * 8, 8)].reshape(256, HS), half, i * 256, 256)
        parts = [(cache[half, 0, sl], cache[half, 1, sl], b) for sl, b in here]
        parts.append((kself[...], rx[0, 2].reshape(VT, HS), None))
        top, total, acc = attend(q, parts)
        ob[0, pl.ds(i * 8, 8)] = (acc / total).astype(jnp.bfloat16).reshape(8, TOK, HS)
        return 0
    lax.fori_loop(0, 2, whole, 0)
    for_peers(lambda t: send_out(0, t))
    own_out(0).start()

    for cp in dc_copies:
        cp.wait()
    c_w.wait()
    pltpu.make_async_copy(frames.at[pl.ds(2, FR)], frames.at[pl.ds(2, FR)], r_dec).wait()
    fview = frames.reshape(5, LT, 64, 128)
    oview = outd.reshape(6, LT, 64, 128)
    lhs = [jnp.concatenate([fview[pl.ds(tap, FR), j].reshape(FR * 64, 128) for j in range(LT)], axis=1) for tap in range(3)]
    for i in range(2):
        n = pl.ds(i * CH, CH)
        conv = dot(lhs[0], weight[0, :, n]) + dot(lhs[1], weight[1, :, n]) + dot(lhs[2], weight[2, :, n])
        conv = (conv + bias_ref[:, n]).astype(jnp.bfloat16)
        for t in range(FR):
            for j in range(LT):
                oview[2 * t + i, j] = conv[t * 64:(t + 1) * 64, j * 128:(j + 1) * 128]
    o_copies = []
    for j in range(LT):
        cp = pltpu.make_async_copy(outd.at[:, j], decoded.at[0, :, :, :, pl.ds(j * 128, 128)], l_out.at[j])
        cp.start()
        o_copies.append(cp)

    pltpu.make_async_copy(rx.at[1, pl.ds(1, 2), pl.ds(0, 15)], rx.at[1, pl.ds(1, 2), pl.ds(0, 15)], r_b).wait()
    rotate_keys(1)

    def merged(i, _):
        q = rotate(rx[1, 0, pl.ds(i * 4, 4)].reshape(128, HS), half, i * 128, 128)
        top, total, acc = attend(q, [(kself[...], rx[1, 2].reshape(VT, HS), None)])
        pltpu.make_async_copy(lse_in.at[i], lse_in.at[i], r_lse.at[i]).wait()
        pltpu.make_async_copy(oc.at[i], oc.at[i], r_oc.at[i]).wait()
        lse = jnp.broadcast_to(lse_in[i, 0:1, :], (128, 128))
        lse = jnp.sum(jnp.where(eye, lse, 0.0), axis=1, keepdims=True)
        both = jnp.maximum(lse, top)
        wc = jnp.exp2(lse - both)
        ws = jnp.exp2(top - both)
        mixed = (oc[i].astype(jnp.float32) * wc + acc * ws) / (wc + total * ws)
        ob[1, pl.ds(i * 4, 4)] = mixed.astype(jnp.bfloat16).reshape(4, TOK, HS)
        return 0
    lax.fori_loop(0, 4, merged, 0)
    for_peers(lambda t: send_out(1, t))
    own_out(1).start()

    own_out(0).wait()
    own_out(1).wait()
    for cp in o_copies:
        cp.wait()
    piece = rx.at[:, :, pl.ds(0, 15)]
    pltpu.make_async_copy(piece, piece, s_send).wait()
    pltpu.make_async_copy(fq, fq, s_fwd).wait()
    pltpu.make_async_copy(oc, oc, s_oc.at[0]).wait()
    pltpu.make_async_copy(lse_in, lse_in, s_oc.at[1]).wait()
    piece = rx.at[:, 0, pl.ds(0, 15)]
    pltpu.make_async_copy(piece, piece, s_o).wait()

    @pl.when(s // 2 != g)
    def _():
        pltpu.make_async_copy(frames.at[pl.ds(2, FR)], frames.at[pl.ds(2, FR)], s_dec).wait()

    @pl.when(s // 2 == g)
    def _():
        part = frames.at[pl.ds(2, FR), :, pl.ds(0, 31)]
        pltpu.make_async_copy(part, part, s_dec).wait()
    pltpu.make_async_copy(piece, piece, r_o).wait()


def on_device(qkv, kv_cache, cycle_slot, valid_count, span_pos, dec_in, dec_cache, time_weight, time_bias):
    f = np.exp(-math.log(10000.0) * np.arange(64, dtype=np.float64) / 64)
    freq = jnp.asarray(np.concatenate([f, f]).astype(np.float32))
    sign = jnp.asarray(np.concatenate([-np.ones(64), np.ones(64)]).astype(np.float32))
    ang = (span_pos * VT).astype(jnp.float32)[:, None] * freq[None, :]
    base = jnp.concatenate([jnp.cos(ang), jnp.sin(ang) * sign[None, :]], 0)
    cos_t, sin_t = rope_tables()
    bf, f32 = jnp.bfloat16, jnp.float32
    vmem, hbm, smem = pltpu.VMEM, pl.BlockSpec(memory_space=pl.ANY), pl.BlockSpec(memory_space=pltpu.SMEM)
    inv = pl.BlockSpec(memory_space=pltpu.VMEM)
    dma = pltpu.SemaphoreType.DMA
    return pl.pallas_call(
        kernel,
        out_shape=(
            jax.ShapeDtypeStruct((TOK, 32 * HS), bf),
            jax.ShapeDtypeStruct((1, 2 * FR, 32, 2, CH), bf),
        ),
        in_specs=[smem, smem, inv, hbm, hbm, hbm, hbm, hbm, inv, hbm, hbm],
        out_specs=(hbm, hbm),
        scratch_shapes=[
            vmem((2, 3, HALF, TOK, HS), bf),
            vmem((HALF, TOK, HS), bf),
            vmem((4, 128, HS), bf),
            vmem((4, 128, HS), bf),
            vmem((4, 8, 128), f32),
            vmem((4, 8, 128), f32),
            vmem((2, HALF, TOK, HS), bf),
            vmem((2, 2, CYCLE, VT, HS), bf),
            vmem((3, CH, 2 * CH), bf),
            vmem((2, VT, HS), f32),
            vmem((2, VT, HS), f32),
            vmem((2, VT, HS), f32),
            vmem((VT, HS), bf),
            vmem((2, FR, LT, 16, 2, 128), bf),
            vmem((5, LT, 32, 2, 128), bf),
            vmem((6, LT, 32, 2, 128), bf),
            dma, dma, dma((2,)), dma, dma,
            dma((HALF,)), dma, dma, dma((4,)), dma((4,)), dma((4,)), dma, dma,
            dma((2,)), dma, dma, dma((2,)), dma((LT,)), dma((2 * LT,)), dma((LT,)),
        ],
        name="rollout",
        compiler_params=pltpu.CompilerParams(collective_id=0, has_side_effects=True, vmem_limit_bytes=48 * 1024 * 1024),
    )(
        cycle_slot, valid_count, base, jnp.transpose(qkv, (1, 0, 2)), kv_cache, dec_in, dec_cache,
        time_weight, time_bias.reshape(1, 2 * CH), jnp.asarray(cos_t), jnp.asarray(sin_t),
    )


def solution(mesh):
    placed = (
        P(("grp", "sp"), None, None),
        P("grp", None, None, None, "sp"),
        P("grp"),
        P("grp"),
        P("grp"),
        P("grp", None, "sp", None, None),
        P("sp", None, None, "grp", None),
        P(),
        P(),
    )
    return jax.shard_map(
        on_device,
        mesh=mesh,
        in_specs=placed,
        out_specs=(P(("grp", "sp"), None), P("sp", None, None, "grp", None)),
        check_vma=False,
    )
```

time: 155 us -> 80.1 us (0.52)
  the two profiles are of different devices: /device:TPU:1 before, /device:TPU:7 now
where the time goes in v1:
time: 80.1 us; the launch traced here: 79.7 us
  Pallas kernels  66.4 us (83%)
  local copies, waits for them, and re-layouts  11.1 us (14%)
  other arithmetic  1.45 us (2%)
    pallas_call x1, Pallas kernels, on_device(): pl.pallas_call(kernel, out_shape=(jax.ShapeDtypeStruct((TOK, 32 * HS), bf...  66.4 us
    unnamed x20, local copies, waits for them, and re-layouts  10.4 us

profile of v1, /device:TPU:7, one launch (start us, length us, event | category | flops | bytes accessed | tf_op | source)
XLA Modules:
  0.0 79.7 jit_solution(2686851244416409959)
XLA Ops:
  0.6 0.7 multiply_convert_fusion
  1.3 0.8 multiply_cosine_fusion
  2.1 0.7 reshape.10.bias_ref
  2.8 0.0 copy-start
  2.8 1.5 %copy-done = bf16[3,384,768]{2,1,0:T(8,128)(2,1)S(1)} copy-done((bf16[3,384,768]{2,1,0:T(8,128)(2,1)S(1)}, bf16[3,384,768]{2,1,0:T(8,128)(2,1)}, u32[]{:S(2)}) %copy-start) | copy-done | bytes 1769496
  4.3 0.0 copy-start.1
  4.3 1.4 %copy-done.1 = bf16[2,2,3,512,128]{4,3,2,1,0:T(8,128)(2,1)S(1)} copy-done((bf16[2,2,3,512,128]{4,3,2,1,0:T(8,128)(2,1)S(1)}, bf16[2,2,3,512,128]{4,3,2,1,0:T(8,128)(2,1)}, u32[]{:S(2)}) %copy-start.1) | copy-done | bytes 1572888
  5.7 0.0 copy-start.2
  5.7 1.1 %copy-done.2 = bf16[32,3,4096]{2,0,1:T(8,128)(2,1)S(1)} copy-done((bf16[32,3,4096]{2,0,1:T(8,128)(2,1)S(1)}, bf16[32,3,4096]{2,0,1:T(8,128)(2,1)}, u32[]{:S(2)}) %copy-start.2) | copy-done | bytes 786456
  6.8 0.0 copy-start.3
  6.8 0.9 %copy-done.3 = f32[512,128]{1,0:T(8,128)S(1)} copy-done((f32[512,128]{1,0:T(8,128)S(1)}, f32[512,128]{1,0:T(8,128)}, u32[]{:S(2)}) %copy-start.3) | copy-done | bytes 262168
  7.7 0.0 copy-start.4
  7.7 0.9 %copy-done.4 = f32[512,128]{1,0:T(8,128)S(1)} copy-done((f32[512,128]{1,0:T(8,128)S(1)}, f32[512,128]{1,0:T(8,128)}, u32[]{:S(2)}) %copy-start.4) | copy-done | bytes 262168
  8.7 0.0 copy-start.5
  8.7 0.9 %copy-done.5 = bf16[2,3,1,32,384]{4,3,2,1,0:T(8,128)(2,1)S(1)} copy-done((bf16[2,3,1,32,384]{4,3,2,1,0:T(8,128)(2,1)S(1)}, bf16[2,3,1,32,384]{4,3,2,1,0:T(8,128)(2,1)}, u32[]{:S(2)}) %copy-start.5) | copy-done | bytes 147480
  9.6 0.0 copy-start.6
  9.6 0.9 %copy-done.6 = bf16[1,2,32,2,384]{4,3,2,1,0:T(2,128)(2,1)S(1)} copy-done((bf16[1,2,32,2,384]{4,3,2,1,0:T(2,128)(2,1)S(1)}, bf16[1,2,32,2,384]{4,3,2,1,0:T(2,128)(2,1)}, u32[]{:S(2)}) %copy-start.6) | copy-done | bytes 98328
  10.5 0.0 copy-start.7
  10.5 0.7 copy-done.7
  11.2 0.0 copy-start.8
  11.2 0.7 copy-done.8
  11.8 66.4 %rollout.1 = (bf16[32,4096]{1,0:T(8,128)(2,1)S(1)}, bf16[1,6,32,2,384]{4,3,2,1,0:T(2,128)(2,1)S(1)}) custom-call(s32[2]{0:T(128)S(1)} %copy-done.7, s32[2]{0:T(128)S(1)} %copy-done.8, f32[4,128]{1,0:T(4,128)S(1)} %pad_maximum_fusion.base_ref, bf16[3,32,4096]{2,1,0:T(8,128)(2,1)S(1)} %bitcast.1, bf16[2,2,3,512,128]{4,3,2,1,0:T(8,128)(2,1)S(1)} %copy-done.1, ...), custom_call_target="tpu_custom_call" | custom-call | tf_op jit(solution)/shard_map/rollout/pallas_call | solution.py:317
  78.3 0.7 copy.17
  79.0 0.7 copy.18
  (1 shorter events, 0.0 us)
Async XLA Ops:
  2.8 1.5 %copy-start = (bf16[3,384,768]{2,1,0:T(8,128)(2,1)S(1)}, bf16[3,384,768]{2,1,0:T(8,128)(2,1)}, u32[]{:S(2)}) copy-start(bf16[3,384,768]{2,1,0:T(8,128)(2,1)} %weight_hbm.1) | copy-start | bytes 5308420
  4.3 1.4 %copy-start.1 = (bf16[2,2,3,512,128]{4,3,2,1,0:T(8,128)(2,1)S(1)}, bf16[2,2,3,512,128]{4,3,2,1,0:T(8,128)(2,1)}, u32[]{:S(2)}) copy-start(bf16[2,2,3,512,128]{4,3,2,1,0:T(8,128)(2,1)} %cache_hbm.1) | copy-start | bytes 4718596
  5.7 1.1 %copy-start.2 = (bf16[32,3,4096]{2,0,1:T(8,128)(2,1)S(1)}, bf16[32,3,4096]{2,0,1:T(8,128)(2,1)}, u32[]{:S(2)}) copy-start(bf16[32,3,4096]{2,0,1:T(8,128)(2,1)} %param.13) | copy-start | bytes 2359300
  6.8 0.9 %copy-start.3 = (f32[512,128]{1,0:T(8,128)S(1)}, f32[512,128]{1,0:T(8,128)}, u32[]{:S(2)}) copy-start(f32[512,128]{1,0:T(8,128)} %constant.13.clone.sin_hbm) | copy-start | bytes 786436
  7.7 0.9 %copy-start.4 = (f32[512,128]{1,0:T(8,128)S(1)}, f32[512,128]{1,0:T(8,128)}, u32[]{:S(2)}) copy-start(f32[512,128]{1,0:T(8,128)} %constant.12.clone.cos_hbm) | copy-start | bytes 786436
  8.7 0.9 %copy-start.5 = (bf16[2,3,1,32,384]{4,3,2,1,0:T(8,128)(2,1)S(1)}, bf16[2,3,1,32,384]{4,3,2,1,0:T(8,128)(2,1)}, u32[]{:S(2)}) copy-start(bf16[2,3,1,32,384]{4,3,2,1,0:T(8,128)(2,1)} %dec_in.1) | copy-start | bytes 442372
  9.6 0.9 %copy-start.6 = (bf16[1,2,32,2,384]{4,3,2,1,0:T(2,128)(2,1)S(1)}, bf16[1,2,32,2,384]{4,3,2,1,0:T(2,128)(2,1)}, u32[]{:S(2)}) copy-start(bf16[1,2,32,2,384]{4,3,2,1,0:T(2,128)(2,1)} %dec_cache.1) | copy-start | bytes 294916
  10.5 0.7 copy-start.7
  11.2 0.7 copy-start.8

commit v2 on v1

--- a/solution.py
+++ b/solution.py
@@ -16,6 +16,7 @@
 HALF = 16
 TOK = 32
 VT = 512
+SPANS = 64
 FR = 3
 CH = 384
 LT = CH // 128
@@ -23,9 +24,10 @@
 
 def rope_tables():
     f = np.exp(-math.log(10000.0) * np.arange(64, dtype=np.float64) / 64)
-    ang = np.arange(VT, dtype=np.float64)[:, None] * np.concatenate([f, f])[None, :]
+    steps = np.concatenate([np.arange(VT), VT * np.arange(SPANS)]).astype(np.float64)
+    ang = steps[:, None] * np.concatenate([f, f])[None, :]
     sign = np.concatenate([-np.ones(64), np.ones(64)])
-    return np.cos(ang).astype(np.float32), (np.sin(ang) * sign).astype(np.float32)
+    return np.stack([np.cos(ang), np.sin(ang) * sign]).astype(np.float32)
 
 
 def dot_t(a, b):
@@ -53,10 +55,10 @@
 
 
 def kernel(
-    slot_ref, count_ref, base_ref, qkv, cache_hbm, dec_in, dec_cache, weight_hbm, bias_ref, cos_hbm, sin_hbm,
+    slot_ref, count_ref, pos_ref, qkv, cache_hbm, dec_in, dec_cache, weight_hbm, bias_hbm, tab_hbm,
     out, decoded,
-    rx, fq, oc, oc_out, lse_in, lse_out, ob, cache, weight, tabs, cosv, sinv, kself, sendd, frames, outd,
-    s_send, s_fwd, s_oc, s_o, s_dec, r_qb, r_a, r_b, r_fq, r_oc, r_lse, r_o, r_dec, l_own, l_cache, l_w, l_tab, l_dc, l_ds, l_out,
+    rx, fq, oc, oc_out, lse_in, lse_out, ob, cache, weight, bias_ref, tabs, cosv, sinv, kself, sendd, mid, frames, outd,
+    s_send, s_fwd, s_oc, s_o, s_dec, r_qb, r_a, r_b, r_fq, r_oc, r_lse, r_o, r_dec, r_mid, l_own, l_cache, l_w, l_bias, l_tab, l_dc, l_ds, l_out,
 ):
     g = lax.axis_index("grp")
     s = lax.axis_index("sp")
@@ -68,7 +70,7 @@
     other = 1 - half
 
     def peer(k, cc):
-        step = (k // 2 + 1) * (1 - 2 * (k % 2))
+        step = jnp.where(k == 0, 4, ((8 - k) // 2) * (1 - 2 * (k % 2)))
         return ((y + step + 8) % 8) * 2 + (c + cc) % 2
 
     def for_peers(fn):
@@ -81,17 +83,18 @@
     bar = pltpu.get_barrier_semaphore()
     for_peers(lambda t: pl.semaphore_signal(bar, 1, device_id=(g, half * HALF + t), device_id_type=MESH))
     pl.semaphore_signal(bar, 1, device_id=(g, partner), device_id_type=MESH)
-    src_g = s // 2
-    mine = (src_g == g).astype(jnp.int32)
+    def near_half(i):
+        return half * 8 + i // 2, (i % 2) * HALF + me
 
     def greet(i, _):
-        pl.semaphore_signal(bar, 1, device_id=(src_g, (s + 1 + i) % 32), device_id_type=MESH)
-        return 0
-    lax.fori_loop(0, 31, greet, 0)
-
-    @pl.when(src_g != g)
-    def _():
-        pl.semaphore_signal(bar, 1, device_id=(src_g, s), device_id_type=MESH)
+        gs, ss = near_half((i + 2 * g) % 16)
+
+        @pl.when(jnp.logical_not((gs == g) & (ss == s)))
+        def _():
+            pl.semaphore_signal(bar, 1, device_id=(gs, ss), device_id_type=MESH)
+        return 0
+    lax.fori_loop(0, 16, greet, 0)
+    mine = (g // 8 == half).astype(jnp.int32)
 
     def cols(h):
         return pl.ds(pl.multiple_of(h * HS, HS), HS)
@@ -100,10 +103,8 @@
     own = [pltpu.make_async_copy(qkv.at[:, :, cols(head[j])], rx.at[j, :, me], l_own.at[j]) for j in range(2)]
     for cp in own:
         cp.start()
-    c_tab = [pltpu.make_async_copy(h, tabs.at[i], l_tab.at[i]) for i, h in enumerate((cos_hbm, sin_hbm))]
-    for cp in c_tab:
-        cp.start()
-    c_ds = pltpu.make_async_copy
+    c_tab = pltpu.make_async_copy(tab_hbm, tabs, l_tab)
+    c_tab.start()
     ds_copies = []
     for v in range(2):
         for j in range(LT):
@@ -114,13 +115,15 @@
     c_cache.start()
     dc_copies = []
     for j in range(LT):
-        cp = pltpu.make_async_copy(dec_cache.at[0, :, :, :, pl.ds(j * 128, 128)], frames.at[pl.ds(0, 2), j], l_dc.at[j])
+        cp = pltpu.make_async_copy(dec_cache.at[0, :, :, :, pl.ds(j * 128, 128)], frames.reshape(5, LT, 32, 2, 128).at[pl.ds(0, 2), j], l_dc.at[j])
         cp.start()
         dc_copies.append(cp)
     c_w = pltpu.make_async_copy(weight_hbm, weight, l_w)
     c_w.start()
-
-    pl.semaphore_wait(bar, 15 + 1 + 32 - mine)
+    c_b = pltpu.make_async_copy(bias_hbm, bias_ref, l_bias)
+    c_b.start()
+
+    pl.semaphore_wait(bar, 15 + 1 + 16 - mine)
 
     def send(part, n, j, t, rsem):
         pltpu.make_async_remote_copy(
@@ -129,39 +132,36 @@
             device_id=(g, half * HALF + t), device_id_type=MESH,
         ).start()
 
+    for cp in ds_copies:
+        cp.wait()
+
+    def send_stage(i, _):
+        gd, sd = (g + i) % 16, (g // 8) * HALF + me
+        src, dst = sendd.at[:, :, :, gd], mid.at[g % 8, :, :, :, half]
+        itself = (gd == g) & (sd == s)
+
+        @pl.when(jnp.logical_not(itself))
+        def _():
+            pltpu.make_async_remote_copy(src, dst, s_dec.at[0], r_mid, device_id=(gd, sd), device_id_type=MESH).start()
+
+        @pl.when(itself)
+        def _():
+            pltpu.make_async_copy(src, dst, r_mid).start()
+        return 0
+
+    lax.fori_loop(0, 16, send_stage, 0)
     for_peers(lambda t: send(0, 1, 1, t, r_qb.at[me]))
     for_peers(lambda t: send(0, 3, 0, t, r_a))
-    for cp in ds_copies:
-        cp.wait()
-
-    def send_frames(gd, v):
-        return pltpu.make_async_remote_copy(
-            sendd.at[v, :, :, gd], frames.at[pl.ds(2, FR), :, s], s_dec, r_dec,
-            device_id=(gd, 2 * g + v), device_id_type=MESH,
-        )
-
-    def send_far(i, _):
-        send_frames((g + 1 + i // 2) % 16, i % 2).start()
-        return 0
-    lax.fori_loop(0, 30, send_far, 0)
-    for v in range(2):
-        @pl.when(s != 2 * g + v)
-        def _():
-            send_frames(g, v).start()
-
-        @pl.when(s == 2 * g + v)
-        def _():
-            pltpu.make_async_copy(sendd.at[v, :, :, g], frames.at[pl.ds(2, FR), :, s], r_dec).start()
     for_peers(lambda t: send(1, 2, 1, t, r_b))
 
-    for cp in c_tab:
-        cp.wait()
+    c_tab.wait()
+    bases = [[tabs[i, pl.ds(VT + pos_ref[v], 1), :] for i in range(2)] for v in range(2)]
 
     def make_tables(i, _):
         rows = pl.ds(pl.multiple_of(i * 128, 128), 128)
         ct, st = tabs[0, rows, :], tabs[1, rows, :]
         for v in range(2):
-            cb, sb = base_ref[pl.ds(v, 1), :], base_ref[pl.ds(2 + v, 1), :]
+            cb, sb = bases[v]
             cosv[v, rows, :] = ct * cb - st * sb
             sinv[v, rows, :] = st * cb + ct * sb
         return 0
@@ -186,6 +186,17 @@
         pltpu.make_async_copy(rx.at[1, 0, t], rx.at[1, 0, t], r_qb.at[t]).wait()
         forward(t)
     for_peers(wait_forward)
+
+    pltpu.make_async_copy(mid, mid, r_mid).wait()
+    fresh = frames.at[pl.ds(2, FR)]
+
+    def send_frames(t):
+        pltpu.make_async_remote_copy(
+            mid.at[t // 2, t % 2], fresh.at[:, :, :, me], s_dec.at[1], r_dec,
+            device_id=(g, half * HALF + t), device_id_type=MESH,
+        ).start()
+    for_peers(send_frames)
+    pltpu.make_async_copy(mid.at[me // 2, me % 2], fresh.at[:, :, :, me], r_dec).start()
 
     eye = lax.broadcasted_iota(jnp.int32, (128, 128), 0) == lax.broadcasted_iota(jnp.int32, (128, 128), 1)
 
@@ -243,14 +254,15 @@
     for cp in dc_copies:
         cp.wait()
     c_w.wait()
-    pltpu.make_async_copy(frames.at[pl.ds(2, FR)], frames.at[pl.ds(2, FR)], r_dec).wait()
+    c_b.wait()
+    pltpu.make_async_copy(fresh, fresh, r_dec).wait()
     fview = frames.reshape(5, LT, 64, 128)
     oview = outd.reshape(6, LT, 64, 128)
     lhs = [jnp.concatenate([fview[pl.ds(tap, FR), j].reshape(FR * 64, 128) for j in range(LT)], axis=1) for tap in range(3)]
     for i in range(2):
         n = pl.ds(i * CH, CH)
         conv = dot(lhs[0], weight[0, :, n]) + dot(lhs[1], weight[1, :, n]) + dot(lhs[2], weight[2, :, n])
-        conv = (conv + bias_ref[:, n]).astype(jnp.bfloat16)
+        conv = (conv + bias_ref[n].reshape(1, CH)).astype(jnp.bfloat16)
         for t in range(FR):
             for j in range(LT):
                 oview[2 * t + i, j] = conv[t * 64:(t + 1) * 64, j * 128:(j + 1) * 128]
@@ -292,27 +304,23 @@
     piece = rx.at[:, 0, pl.ds(0, 15)]
     pltpu.make_async_copy(piece, piece, s_o).wait()
 
-    @pl.when(s // 2 != g)
+    part = frames.at[pl.ds(2, FR), :, :, pl.ds(0, 15)]
+    pltpu.make_async_copy(part, part, s_dec.at[1]).wait()
+
+    @pl.when(g // 8 != half)
     def _():
-        pltpu.make_async_copy(frames.at[pl.ds(2, FR)], frames.at[pl.ds(2, FR)], s_dec).wait()
-
-    @pl.when(s // 2 == g)
+        pltpu.make_async_copy(sendd, sendd, s_dec.at[0]).wait()
+
+    @pl.when(g // 8 == half)
     def _():
-        part = frames.at[pl.ds(2, FR), :, pl.ds(0, 31)]
-        pltpu.make_async_copy(part, part, s_dec).wait()
+        part = sendd.at[:, :, :, pl.ds(0, 15)]
+        pltpu.make_async_copy(part, part, s_dec.at[0]).wait()
     pltpu.make_async_copy(piece, piece, r_o).wait()
 
 
 def on_device(qkv, kv_cache, cycle_slot, valid_count, span_pos, dec_in, dec_cache, time_weight, time_bias):
-    f = np.exp(-math.log(10000.0) * np.arange(64, dtype=np.float64) / 64)
-    freq = jnp.asarray(np.concatenate([f, f]).astype(np.float32))
-    sign = jnp.asarray(np.concatenate([-np.ones(64), np.ones(64)]).astype(np.float32))
-    ang = (span_pos * VT).astype(jnp.float32)[:, None] * freq[None, :]
-    base = jnp.concatenate([jnp.cos(ang), jnp.sin(ang) * sign[None, :]], 0)
-    cos_t, sin_t = rope_tables()
     bf, f32 = jnp.bfloat16, jnp.float32
     vmem, hbm, smem = pltpu.VMEM, pl.BlockSpec(memory_space=pl.ANY), pl.BlockSpec(memory_space=pltpu.SMEM)
-    inv = pl.BlockSpec(memory_space=pltpu.VMEM)
     dma = pltpu.SemaphoreType.DMA
     return pl.pallas_call(
         kernel,
@@ -320,7 +328,7 @@
             jax.ShapeDtypeStruct((TOK, 32 * HS), bf),
             jax.ShapeDtypeStruct((1, 2 * FR, 32, 2, CH), bf),
         ),
-        in_specs=[smem, smem, inv, hbm, hbm, hbm, hbm, hbm, inv, hbm, hbm],
+        in_specs=[smem, smem, smem] + [hbm] * 7,
         out_specs=(hbm, hbm),
         scratch_shapes=[
             vmem((2, 3, HALF, TOK, HS), bf),
@@ -332,22 +340,24 @@
             vmem((2, HALF, TOK, HS), bf),
             vmem((2, 2, CYCLE, VT, HS), bf),
             vmem((3, CH, 2 * CH), bf),
-            vmem((2, VT, HS), f32),
+            vmem((2 * CH,), f32),
+            vmem((2, VT + SPANS, HS), f32),
             vmem((2, VT, HS), f32),
             vmem((2, VT, HS), f32),
             vmem((VT, HS), bf),
             vmem((2, FR, LT, 16, 2, 128), bf),
-            vmem((5, LT, 32, 2, 128), bf),
+            vmem((8, 2, FR, LT, 2, 2, 128), bf),
+            vmem((5, LT, 2, 16, 2, 128), bf),
             vmem((6, LT, 32, 2, 128), bf),
-            dma, dma, dma((2,)), dma, dma,
-            dma((HALF,)), dma, dma, dma((4,)), dma((4,)), dma((4,)), dma, dma,
-            dma((2,)), dma, dma, dma((2,)), dma((LT,)), dma((2 * LT,)), dma((LT,)),
+            dma, dma, dma((2,)), dma, dma((2,)),
+            dma((HALF,)), dma, dma, dma((4,)), dma((4,)), dma((4,)), dma, dma, dma,
+            dma((2,)), dma, dma, dma, dma, dma((LT,)), dma((2 * LT,)), dma((LT,)),
         ],
         name="rollout",
-        compiler_params=pltpu.CompilerParams(collective_id=0, has_side_effects=True, vmem_limit_bytes=48 * 1024 * 1024),
+        compiler_params=pltpu.CompilerParams(collective_id=0, has_side_effects=True, vmem_limit_bytes=67043328),
     )(
-        cycle_slot, valid_count, base, jnp.transpose(qkv, (1, 0, 2)), kv_cache, dec_in, dec_cache,
-        time_weight, time_bias.reshape(1, 2 * CH), jnp.asarray(cos_t), jnp.asarray(sin_t),
+        cycle_slot, valid_count, span_pos, jnp.transpose(qkv, (1, 0, 2)), kv_cache, dec_in, dec_cache,
+        time_weight, time_bias, jnp.asarray(rope_tables()),
     )
 
 

time: 80.1 us -> 52.9 us (0.66)
  the two profiles are of different devices: /device:TPU:7 before, /device:TPU:1 now
where the time goes in v2:
time: 52.9 us; the launch traced here: 52.2 us
  Pallas kernels  48 us (91%)
  local copies, waits for them, and re-layouts  3.55 us (7%)
  between operations  0.64 us (1%)
    pallas_call x1, Pallas kernels, on_device(): pl.pallas_call(kernel, out_shape=(jax.ShapeDtypeStruct((TOK, 32 * HS), bf...  48 us
    unnamed x2, local copies, waits for them, and re-layouts  3.55 us

profile of v2, /device:TPU:1, one launch (start us, length us, event | category | flops | bytes accessed | tf_op | source)
XLA Modules:
  0.0 52.2 jit_solution(10395229734255677914)
XLA Ops:
  0.6 48.0 %rollout.1 = (bf16[32,4096]{1,0:T(8,128)(2,1)}, bf16[1,6,32,2,384]{4,3,2,1,0:T(2,128)(2,1)}) custom-call(s32[2]{0:T(128)} %slot_ref.1, s32[2]{0:T(128)} %count_ref.1, s32[2]{0:T(128)} %pos_ref.1, bf16[3,32,4096]{2,1,0:T(8,128)(2,1)} %bitcast.1, bf16[2,2,3,512,128]{4,3,2,1,0:T(8,128)(2,1)} %cache_hbm.1, bf16[2,3,1,32,384]{4,3,2,1,0:T(8,128)(2,1)} %dec_in.1, ...), custom_call_target="tpu_custom_call" | custom-call | tf_op jit(solution)/shard_map/rollout/pallas_call | solution.py:325
  48.7 1.7 %copy.14 = bf16[32,4096]{1,0:T(8,128)(2,1)} copy(bf16[32,4096]{1,0:T(8,128)(2,1)} %get-tuple-element.4) | data formatting | bytes 524288
  50.3 1.9 %copy.15 = bf16[1,6,32,2,384]{4,3,2,1,0:T(2,128)(2,1)} copy(bf16[1,6,32,2,384]{4,3,2,1,0:T(2,128)(2,1)} %get-tuple-element.5) | data formatting | bytes 589824

commit v3 on v2

--- a/solution.py
+++ b/solution.py
@@ -55,10 +55,10 @@
 
 
 def kernel(
-    slot_ref, count_ref, pos_ref, qkv, cache_hbm, dec_in, dec_cache, weight_hbm, bias_hbm, tab_hbm,
+    slot_hbm, count_hbm, pos_hbm, qkv, cache_hbm, dec_in, dec_cache, weight_hbm, bias_hbm, tab_hbm,
     out, decoded,
-    rx, fq, oc, oc_out, lse_in, lse_out, ob, cache, weight, bias_ref, tabs, cosv, sinv, kself, sendd, mid, frames, outd,
-    s_send, s_fwd, s_oc, s_o, s_dec, r_qb, r_a, r_b, r_fq, r_oc, r_lse, r_o, r_dec, r_mid, l_own, l_cache, l_w, l_bias, l_tab, l_dc, l_ds, l_out,
+    slot_ref, count_ref, pos_ref, rx, fq, oc, oc_out, lse_in, lse_out, ob, cache, weight, bias_ref, tabs, cosv, sinv, kself, sendd, mid, frames, outd,
+    s_send, s_fwd, s_oc, s_o, s_dec, r_qb, r_a, r_b, r_fq, r_oc, r_lse, r_o, r_dec, r_mid, l_state, l_own, l_cache, l_w, l_bias, l_tab, l_dc, l_ds, l_out,
 ):
     g = lax.axis_index("grp")
     s = lax.axis_index("sp")
@@ -102,6 +102,12 @@
     head = (s, partner)
     own = [pltpu.make_async_copy(qkv.at[:, :, cols(head[j])], rx.at[j, :, me], l_own.at[j]) for j in range(2)]
     for cp in own:
+        cp.start()
+    c_state = [
+        pltpu.make_async_copy(h, r, l_state.at[i])
+        for i, (h, r) in enumerate(((slot_hbm, slot_ref), (count_hbm, count_ref), (pos_hbm, pos_ref)))
+    ]
+    for cp in c_state:
         cp.start()
     c_tab = pltpu.make_async_copy(tab_hbm, tabs, l_tab)
     c_tab.start()
@@ -155,6 +161,8 @@
     for_peers(lambda t: send(1, 2, 1, t, r_b))
 
     c_tab.wait()
+    for cp in c_state:
+        cp.wait()
     bases = [[tabs[i, pl.ds(VT + pos_ref[v], 1), :] for i in range(2)] for v in range(2)]
 
     def make_tables(i, _):
@@ -250,6 +258,26 @@
     lax.fori_loop(0, 2, whole, 0)
     for_peers(lambda t: send_out(0, t))
     own_out(0).start()
+
+    pltpu.make_async_copy(rx.at[1, pl.ds(1, 2), pl.ds(0, 15)], rx.at[1, pl.ds(1, 2), pl.ds(0, 15)], r_b).wait()
+    rotate_keys(1)
+
+    def merged(i, _):
+        q = rotate(rx[1, 0, pl.ds(i * 4, 4)].reshape(128, HS), half, i * 128, 128)
+        top, total, acc = attend(q, [(kself[...], rx[1, 2].reshape(VT, HS), None)])
+        pltpu.make_async_copy(lse_in.at[i], lse_in.at[i], r_lse.at[i]).wait()
+        pltpu.make_async_copy(oc.at[i], oc.at[i], r_oc.at[i]).wait()
+        lse = jnp.broadcast_to(lse_in[i, 0:1, :], (128, 128))
+        lse = jnp.sum(jnp.where(eye, lse, 0.0), axis=1, keepdims=True)
+        both = jnp.maximum(lse, top)
+        wc = jnp.exp2(lse - both)
+        ws = jnp.exp2(top - both)
+        mixed = (oc[i].astype(jnp.float32) * wc + acc * ws) / (wc + total * ws)
+        ob[1, pl.ds(i * 4, 4)] = mixed.astype(jnp.bfloat16).reshape(4, TOK, HS)
+        return 0
+    lax.fori_loop(0, 4, merged, 0)
+    for_peers(lambda t: send_out(1, t))
+    own_out(1).start()
 
     for cp in dc_copies:
         cp.wait()
@@ -272,26 +300,6 @@
         cp.start()
         o_copies.append(cp)
 
-    pltpu.make_async_copy(rx.at[1, pl.ds(1, 2), pl.ds(0, 15)], rx.at[1, pl.ds(1, 2), pl.ds(0, 15)], r_b).wait()
-    rotate_keys(1)
-
-    def merged(i, _):
-        q = rotate(rx[1, 0, pl.ds(i * 4, 4)].reshape(128, HS), half, i * 128, 128)
-        top, total, acc = attend(q, [(kself[...], rx[1, 2].reshape(VT, HS), None)])
-        pltpu.make_async_copy(lse_in.at[i], lse_in.at[i], r_lse.at[i]).wait()
-        pltpu.make_async_copy(oc.at[i], oc.at[i], r_oc.at[i]).wait()
-        lse = jnp.broadcast_to(lse_in[i, 0:1, :], (128, 128))
-        lse = jnp.sum(jnp.where(eye, lse, 0.0), axis=1, keepdims=True)
-        both = jnp.maximum(lse, top)
-        wc = jnp.exp2(lse - both)
-        ws = jnp.exp2(top - both)
-        mixed = (oc[i].astype(jnp.float32) * wc + acc * ws) / (wc + total * ws)
-        ob[1, pl.ds(i * 4, 4)] = mixed.astype(jnp.bfloat16).reshape(4, TOK, HS)
-        return 0
-    lax.fori_loop(0, 4, merged, 0)
-    for_peers(lambda t: send_out(1, t))
-    own_out(1).start()
-
     own_out(0).wait()
     own_out(1).wait()
     for cp in o_copies:
@@ -318,19 +326,34 @@
     pltpu.make_async_copy(piece, piece, r_o).wait()
 
 
+def put_out(a, b, a_out, b_out, sem):
+    copies = [pltpu.make_async_copy(x, o, sem.at[i]) for i, (x, o) in enumerate(((a, a_out), (b, b_out)))]
+    for cp in copies:
+        cp.start()
+    for cp in copies:
+        cp.wait()
+
+
 def on_device(qkv, kv_cache, cycle_slot, valid_count, span_pos, dec_in, dec_cache, time_weight, time_bias):
     bf, f32 = jnp.bfloat16, jnp.float32
-    vmem, hbm, smem = pltpu.VMEM, pl.BlockSpec(memory_space=pl.ANY), pl.BlockSpec(memory_space=pltpu.SMEM)
+    hbm, free = pl.BlockSpec(memory_space=pltpu.MemorySpace.HBM), pl.BlockSpec(memory_space=pl.ANY)
+    vmem, smem = pltpu.VMEM, pltpu.SMEM
     dma = pltpu.SemaphoreType.DMA
-    return pl.pallas_call(
+    operands = (
+        cycle_slot, valid_count, span_pos, jnp.transpose(qkv, (1, 0, 2)), kv_cache, dec_in, dec_cache,
+        time_weight, time_bias, jnp.asarray(rope_tables()),
+    )
+    shapes = (
+        jax.ShapeDtypeStruct((TOK, 32 * HS), bf),
+        jax.ShapeDtypeStruct((1, 2 * FR, 32, 2, CH), bf),
+    )
+    results = pl.pallas_call(
         kernel,
-        out_shape=(
-            jax.ShapeDtypeStruct((TOK, 32 * HS), bf),
-            jax.ShapeDtypeStruct((1, 2 * FR, 32, 2, CH), bf),
-        ),
-        in_specs=[smem, smem, smem] + [hbm] * 7,
-        out_specs=(hbm, hbm),
+        out_shape=shapes,
+        in_specs=[hbm] * 10,
+        out_specs=(free, free),
         scratch_shapes=[
+            smem((2,), jnp.int32), smem((2,), jnp.int32), smem((2,), jnp.int32),
             vmem((2, 3, HALF, TOK, HS), bf),
             vmem((HALF, TOK, HS), bf),
             vmem((4, 128, HS), bf),
@@ -351,14 +374,22 @@
             vmem((6, LT, 32, 2, 128), bf),
             dma, dma, dma((2,)), dma, dma((2,)),
             dma((HALF,)), dma, dma, dma((4,)), dma((4,)), dma((4,)), dma, dma, dma,
-            dma((2,)), dma, dma, dma, dma, dma((LT,)), dma((2 * LT,)), dma((LT,)),
+            dma((3,)), dma((2,)), dma, dma, dma, dma, dma((LT,)), dma((2 * LT,)), dma((LT,)),
         ],
         name="rollout",
-        compiler_params=pltpu.CompilerParams(collective_id=0, has_side_effects=True, vmem_limit_bytes=67043328),
+        compiler_params=pltpu.CompilerParams(collective_id=0, has_side_effects=True, vmem_limit_bytes=20 * 1024 * 1024),
     )(
-        cycle_slot, valid_count, span_pos, jnp.transpose(qkv, (1, 0, 2)), kv_cache, dec_in, dec_cache,
-        time_weight, time_bias, jnp.asarray(rope_tables()),
+        *(pltpu.with_memory_space_constraint(x, pltpu.MemorySpace.HBM) for x in operands)
     )
+    return pl.pallas_call(
+        put_out,
+        out_shape=shapes,
+        in_specs=[free, free],
+        out_specs=(hbm, hbm),
+        scratch_shapes=[dma((2,))],
+        name="put_out",
+        compiler_params=pltpu.CompilerParams(vmem_limit_bytes=1024 * 1024),
+    )(*results)
 
 
 def solution(mesh):

time: 52.9 us -> 48.9 us (0.924)
  the two profiles are of different devices: /device:TPU:1 before, /device:TPU:71 now
where the time goes in v3:
time: 48.9 us; the launch traced here: 48.8 us
  Pallas kernels  48.1 us (98%)
  between operations  0.64 us (1%)
    pallas_call x1, Pallas kernels, on_device(): pl.pallas_call(kernel, out_shape=shapes, in_specs=[hbm] * 10, out_specs=(...  47.3 us

profile of v3, /device:TPU:71, one launch (start us, length us, event | category | flops | bytes accessed | tf_op | source)
XLA Modules:
  0.0 48.8 jit_solution(647710847742102126)
XLA Ops:
  0.6 47.3 %rollout.1 = (bf16[32,4096]{1,0:T(8,128)(2,1)S(1)}, bf16[1,6,32,2,384]{4,3,2,1,0:T(2,128)(2,1)S(1)}) custom-call(s32[2]{0:T(128)} %slot_hbm.1, s32[2]{0:T(128)} %count_hbm.1, s32[2]{0:T(128)} %pos_hbm.1, bf16[3,32,4096]{2,1,0:T(8,128)(2,1)} %bitcast.1, bf16[2,2,3,512,128]{4,3,2,1,0:T(8,128)(2,1)} %cache_hbm.1, bf16[2,3,1,32,384]{4,3,2,1,0:T(8,128)(2,1)} %dec_in.1, ...), custom_call_target="tpu_custom_call" | custom-call | tf_op jit(solution)/shard_map/rollout/pallas_call | solution.py:350
  47.9 0.8 %put_out.1 = (bf16[32,4096]{1,0:T(8,128)(2,1)}, bf16[1,6,32,2,384]{4,3,2,1,0:T(2,128)(2,1)}) custom-call(bf16[32,4096]{1,0:T(8,128)(2,1)S(1)} %get-tuple-element.4.a, bf16[1,6,32,2,384]{4,3,2,1,0:T(2,128)(2,1)S(1)} %get-tuple-element.5.b), custom_call_target="tpu_custom_call" | custom-call | tf_op jit(solution)/shard_map/put_out/pallas_call | solution.py:384

commit v4 on v3

--- a/solution.py
+++ b/solution.py
@@ -82,19 +82,13 @@
 
     bar = pltpu.get_barrier_semaphore()
     for_peers(lambda t: pl.semaphore_signal(bar, 1, device_id=(g, half * HALF + t), device_id_type=MESH))
-    pl.semaphore_signal(bar, 1, device_id=(g, partner), device_id_type=MESH)
-    def near_half(i):
-        return half * 8 + i // 2, (i % 2) * HALF + me
-
     def greet(i, _):
-        gs, ss = near_half((i + 2 * g) % 16)
-
-        @pl.when(jnp.logical_not((gs == g) & (ss == s)))
-        def _():
-            pl.semaphore_signal(bar, 1, device_id=(gs, ss), device_id_type=MESH)
+        pl.semaphore_signal(bar, 1, device_id=((g + 1 + i) % 16, s), device_id_type=MESH)
         return 0
-    lax.fori_loop(0, 16, greet, 0)
-    mine = (g // 8 == half).astype(jnp.int32)
+
+    @pl.when(half == 1)
+    def _():
+        lax.fori_loop(0, 15, greet, 0)
 
     def cols(h):
         return pl.ds(pl.multiple_of(h * HS, HS), HS)
@@ -129,7 +123,19 @@
     c_b = pltpu.make_async_copy(bias_hbm, bias_ref, l_bias)
     c_b.start()
 
-    pl.semaphore_wait(bar, 15 + 1 + 16 - mine)
+    pl.semaphore_wait(bar, 15 + 31 * half)
+
+    def report(i, _):
+        pl.semaphore_signal(bar, 1, device_id=((g + i) % 16, partner), device_id_type=MESH)
+        return 0
+
+    @pl.when(half == 0)
+    def _():
+        lax.fori_loop(0, 16, report, 0)
+
+    @pl.when(half == 1)
+    def _():
+        pl.semaphore_signal(bar, 1, device_id=(g, partner), device_id_type=MESH)
 
     def send(part, n, j, t, rsem):
         pltpu.make_async_remote_copy(
@@ -138,24 +144,6 @@
             device_id=(g, half * HALF + t), device_id_type=MESH,
         ).start()
 
-    for cp in ds_copies:
-        cp.wait()
-
-    def send_stage(i, _):
-        gd, sd = (g + i) % 16, (g // 8) * HALF + me
-        src, dst = sendd.at[:, :, :, gd], mid.at[g % 8, :, :, :, half]
-        itself = (gd == g) & (sd == s)
-
-        @pl.when(jnp.logical_not(itself))
-        def _():
-            pltpu.make_async_remote_copy(src, dst, s_dec.at[0], r_mid, device_id=(gd, sd), device_id_type=MESH).start()
-
-        @pl.when(itself)
-        def _():
-            pltpu.make_async_copy(src, dst, r_mid).start()
-        return 0
-
-    lax.fori_loop(0, 16, send_stage, 0)
     for_peers(lambda t: send(0, 1, 1, t, r_qb.at[me]))
     for_peers(lambda t: send(0, 3, 0, t, r_a))
     for_peers(lambda t: send(1, 2, 1, t, r_b))
@@ -180,6 +168,29 @@
         rows = pl.ds(pl.multiple_of(row, n), n)
         return (x * cosv[v, rows, :] + pltpu.roll(x, 64, 1) * sinv[v, rows, :]).astype(jnp.bfloat16)
 
+    @pl.when(half == 0)
+    def _():
+        pl.semaphore_wait(bar, 1)
+
+    for cp in ds_copies:
+        cp.wait()
+
+    def send_stage(i, _):
+        gd, sd = (g + i) % 16, (g // 8) * HALF + me
+        src, dst = sendd.at[:, :, :, gd], mid.at[g % 8, :, :, :, half]
+        itself = (gd == g) & (sd == s)
+
+        @pl.when(jnp.logical_not(itself))
+        def _():
+            pltpu.make_async_remote_copy(src, dst, s_dec.at[0], r_mid, device_id=(gd, sd), device_id_type=MESH).start()
+
+        @pl.when(itself)
+        def _():
+            pltpu.make_async_copy(src, dst, r_mid).start()
+        return 0
+
+    lax.fori_loop(0, 16, send_stage, 0)
+
     def forward(t):
         pltpu.make_async_remote_copy(
             rx.at[1, 0, t], fq.at[t], s_fwd, r_fq.at[t // 4],
@@ -194,6 +205,82 @@
         pltpu.make_async_copy(rx.at[1, 0, t], rx.at[1, 0, t], r_qb.at[t]).wait()
         forward(t)
     for_peers(wait_forward)
+
+    eye = lax.broadcasted_iota(jnp.int32, (128, 128), 0) == lax.broadcasted_iota(jnp.int32, (128, 128), 1)
+
+    def slots(v):
+        cs, vc = slot_ref[v], count_ref[v]
+        s0 = jnp.where(cs == 0, 1, 0)
+        s1 = jnp.where(cs == 2, 1, 2)
+        return [(sl, jnp.where(sl < vc, 0.0, NEG)) for sl in (s0, s1)]
+
+    def send_out(j, t):
+        pltpu.make_async_remote_copy(
+            ob.at[j, t], out.at[:, cols(head[j])], s_o, r_o,
+            device_id=(g, half * HALF + t), device_id_type=MESH,
+        ).start()
+
+    def own_out(j):
+        return pltpu.make_async_copy(ob.at[j, me], out.at[:, cols(head[j])], l_own.at[j])
+
+    def rotate_keys(j):
+        def body(i, _):
+            kself[pl.ds(pl.multiple_of(i * 128, 128), 128), :] = rotate(rx[j, 1, pl.ds(i * 4, 4)].reshape(128, HS), half, i * 128, 128)
+            return 0
+        lax.fori_loop(0, 4, body, 0)
+
+    def far_chunk(k):
+        return (k + y // 2 + 2) % 4
+
+    def serve_partner():
+        there = slots(other)
+
+        def cross(k, _):
+            i = far_chunk(k)
+            pltpu.make_async_copy(fq.at[pl.ds(i * 4, 4)], fq.at[pl.ds(i * 4, 4)], r_fq.at[i]).wait()
+            q = rotate(fq[pl.ds(i * 4, 4)].reshape(128, HS), other, i * 128, 128)
+            top, total, acc = attend(q, [(cache[other, 0, sl], cache[other, 1, sl], b) for sl, b in there])
+            oc_out[i] = (acc / total).astype(jnp.bfloat16)
+            lse = jnp.broadcast_to(top + jnp.log2(total), (128, 128))
+            lse_out[i] = jnp.broadcast_to(jnp.sum(jnp.where(eye, lse, 0.0), axis=0, keepdims=True), (8, 128))
+            pltpu.make_async_remote_copy(oc_out.at[i], oc.at[i], s_oc.at[0], r_oc.at[i], device_id=(g, partner), device_id_type=MESH).start()
+            pltpu.make_async_remote_copy(lse_out.at[i], lse_in.at[i], s_oc.at[1], r_lse.at[i], device_id=(g, partner), device_id_type=MESH).start()
+            return 0
+        lax.fori_loop(0, 4, cross, 0)
+
+    def own_head():
+        pltpu.make_async_copy(rx.at[0, :, pl.ds(0, 15)], rx.at[0, :, pl.ds(0, 15)], r_a).wait()
+        here = slots(half)
+        rotate_keys(0)
+
+        def whole(i, _):
+            q = rotate(rx[0, 0, pl.ds(i * 8, 8)].reshape(256, HS), half, i * 256, 256)
+            parts = [(cache[half, 0, sl], cache[half, 1, sl], b) for sl, b in here]
+            parts.append((kself[...], rx[0, 2].reshape(VT, HS), None))
+            top, total, acc = attend(q, parts)
+            ob[0, pl.ds(i * 8, 8)] = (acc / total).astype(jnp.bfloat16).reshape(8, TOK, HS)
+            return 0
+        lax.fori_loop(0, 2, whole, 0)
+        for_peers(lambda t: send_out(0, t))
+        own_out(0).start()
+
+    c_cache.wait()
+
+    @pl.when(half == 1)
+    def _():
+        serve_partner()
+
+    @pl.when(half == 0)
+    def _():
+        own_head()
+
+    @pl.when(half == 1)
+    def _():
+        own_head()
+
+    @pl.when(half == 0)
+    def _():
+        serve_partner()
 
     pltpu.make_async_copy(mid, mid, r_mid).wait()
     fresh = frames.at[pl.ds(2, FR)]
@@ -206,63 +293,11 @@
     for_peers(send_frames)
     pltpu.make_async_copy(mid.at[me // 2, me % 2], fresh.at[:, :, :, me], r_dec).start()
 
-    eye = lax.broadcasted_iota(jnp.int32, (128, 128), 0) == lax.broadcasted_iota(jnp.int32, (128, 128), 1)
-
-    def slots(v):
-        cs, vc = slot_ref[v], count_ref[v]
-        s0 = jnp.where(cs == 0, 1, 0)
-        s1 = jnp.where(cs == 2, 1, 2)
-        return [(sl, jnp.where(sl < vc, 0.0, NEG)) for sl in (s0, s1)]
-
-    c_cache.wait()
-    there = slots(other)
-
-    def cross(i, _):
-        pltpu.make_async_copy(fq.at[pl.ds(i * 4, 4)], fq.at[pl.ds(i * 4, 4)], r_fq.at[i]).wait()
-        q = rotate(fq[pl.ds(i * 4, 4)].reshape(128, HS), other, i * 128, 128)
-        top, total, acc = attend(q, [(cache[other, 0, sl], cache[other, 1, sl], b) for sl, b in there])
-        oc_out[i] = (acc / total).astype(jnp.bfloat16)
-        lse = jnp.broadcast_to(top + jnp.log2(total), (128, 128))
-        lse_out[i] = jnp.broadcast_to(jnp.sum(jnp.where(eye, lse, 0.0), axis=0, keepdims=True), (8, 128))
-        pltpu.make_async_remote_copy(oc_out.at[i], oc.at[i], s_oc.at[0], r_oc.at[i], device_id=(g, partner), device_id_type=MESH).start()
-        pltpu.make_async_remote_copy(lse_out.at[i], lse_in.at[i], s_oc.at[1], r_lse.at[i], device_id=(g, partner), device_id_type=MESH).start()
-        return 0
-    lax.fori_loop(0, 4, cross, 0)
-
-    def send_out(j, t):
-        pltpu.make_async_remote_copy(
-            ob.at[j, t], out.at[:, cols(head[j])], s_o, r_o,
-            device_id=(g, half * HALF + t), device_id_type=MESH,
-        ).start()
-
-    def own_out(j):
-        return pltpu.make_async_copy(ob.at[j, me], out.at[:, cols(head[j])], l_own.at[j])
-
-    def rotate_keys(j):
-        def body(i, _):
-            kself[pl.ds(pl.multiple_of(i * 128, 128), 128), :] = rotate(rx[j, 1, pl.ds(i * 4, 4)].reshape(128, HS), half, i * 128, 128)
-            return 0
-        lax.fori_loop(0, 4, body, 0)
-
-    pltpu.make_async_copy(rx.at[0, :, pl.ds(0, 15)], rx.at[0, :, pl.ds(0, 15)], r_a).wait()
-    here = slots(half)
-    rotate_keys(0)
-
-    def whole(i, _):
-        q = rotate(rx[0, 0, pl.ds(i * 8, 8)].reshape(256, HS), half, i * 256, 256)
-        parts = [(cache[half, 0, sl], cache[half, 1, sl], b) for sl, b in here]
-        parts.append((kself[...], rx[0, 2].reshape(VT, HS), None))
-        top, total, acc = attend(q, parts)
-        ob[0, pl.ds(i * 8, 8)] = (acc / total).astype(jnp.bfloat16).reshape(8, TOK, HS)
-        return 0
-    lax.fori_loop(0, 2, whole, 0)
-    for_peers(lambda t: send_out(0, t))
-    own_out(0).start()
-
     pltpu.make_async_copy(rx.at[1, pl.ds(1, 2), pl.ds(0, 15)], rx.at[1, pl.ds(1, 2), pl.ds(0, 15)], r_b).wait()
     rotate_keys(1)
 
-    def merged(i, _):
+    def merged(k, _):
+        i = far_chunk(k)
         q = rotate(rx[1, 0, pl.ds(i * 4, 4)].reshape(128, HS), half, i * 128, 128)
         top, total, acc = attend(q, [(kself[...], rx[1, 2].reshape(VT, HS), None)])
         pltpu.make_async_copy(lse_in.at[i], lse_in.at[i], r_lse.at[i]).wait()
@@ -274,10 +309,21 @@
         ws = jnp.exp2(top - both)
         mixed = (oc[i].astype(jnp.float32) * wc + acc * ws) / (wc + total * ws)
         ob[1, pl.ds(i * 4, 4)] = mixed.astype(jnp.bfloat16).reshape(4, TOK, HS)
+
+        def hand_out(b, _):
+            t = i * 4 + b
+
+            @pl.when(t != me)
+            def _():
+                send_out(1, t)
+
+            @pl.when(t == me)
+            def _():
+                own_out(1).start()
+            return 0
+        lax.fori_loop(0, 4, hand_out, 0)
         return 0
     lax.fori_loop(0, 4, merged, 0)
-    for_peers(lambda t: send_out(1, t))
-    own_out(1).start()
 
     for cp in dc_copies:
         cp.wait()

time: 48.9 us -> 43.4 us (0.89)
  the two profiles are of different devices: /device:TPU:71 before, /device:TPU:1 now
where the time goes in v4:
time: 43.4 us; the launch traced here: 43.3 us
  Pallas kernels  42.6 us (98%)
  between operations  0.64 us (1%)
    pallas_call x1, Pallas kernels, on_device(): pl.pallas_call(kernel, out_shape=shapes, in_specs=[hbm] * 10, out_specs=(...  41.8 us

profile of v4, /device:TPU:1, one launch (start us, length us, event | category | flops | bytes accessed | tf_op | source)
XLA Modules:
  0.0 43.3 jit_solution(17032806425934597942)
XLA Ops:
  0.6 41.8 %rollout.1 = (bf16[32,4096]{1,0:T(8,128)(2,1)S(1)}, bf16[1,6,32,2,384]{4,3,2,1,0:T(2,128)(2,1)S(1)}) custom-call(s32[2]{0:T(128)} %slot_hbm.1, s32[2]{0:T(128)} %count_hbm.1, s32[2]{0:T(128)} %pos_hbm.1, bf16[3,32,4096]{2,1,0:T(8,128)(2,1)} %bitcast.1, bf16[2,2,3,512,128]{4,3,2,1,0:T(8,128)(2,1)} %cache_hbm.1, bf16[2,3,1,32,384]{4,3,2,1,0:T(8,128)(2,1)} %dec_in.1, ...), custom_call_target="tpu_custom_call" | custom-call | tf_op jit(solution)/shard_map/rollout/pallas_call | solution.py:396
  42.5 0.8 %put_out.1 = (bf16[32,4096]{1,0:T(8,128)(2,1)}, bf16[1,6,32,2,384]{4,3,2,1,0:T(2,128)(2,1)}) custom-call(bf16[32,4096]{1,0:T(8,128)(2,1)S(1)} %get-tuple-element.4.a, bf16[1,6,32,2,384]{4,3,2,1,0:T(2,128)(2,1)S(1)} %get-tuple-element.5.b), custom_call_target="tpu_custom_call" | custom-call | tf_op jit(solution)/shard_map/put_out/pallas_call | solution.py:430

commit v5 on v4

--- a/solution.py
+++ b/solution.py
@@ -189,7 +189,9 @@
             pltpu.make_async_copy(src, dst, r_mid).start()
         return 0
 
-    lax.fori_loop(0, 16, send_stage, 0)
+    @pl.when((half == 1) | (g // 8 == 0))
+    def _():
+        lax.fori_loop(0, 16, send_stage, 0)
 
     def forward(t):
         pltpu.make_async_remote_copy(
@@ -199,12 +201,31 @@
 
     for cp in own:
         cp.wait()
-    forward(me)
+    def far_chunk(k):
+        return (k + y // 2 + 2) % 4
 
     def wait_forward(t):
-        pltpu.make_async_copy(rx.at[1, 0, t], rx.at[1, 0, t], r_qb.at[t]).wait()
+        @pl.when(t != me)
+        def _():
+            pltpu.make_async_copy(rx.at[1, 0, t], rx.at[1, 0, t], r_qb.at[t]).wait()
         forward(t)
-    for_peers(wait_forward)
+
+    def forward_chunks(k, _):
+        wait_forward(far_chunk(k // 4) * 4 + k % 4)
+        return 0
+
+    @pl.when(half == 0)
+    def _():
+        lax.fori_loop(0, 16, forward_chunks, 0)
+
+    @pl.when(half == 1)
+    def _():
+        forward(me)
+        for_peers(wait_forward)
+
+    @pl.when((half == 0) & (g // 8 == 1))
+    def _():
+        lax.fori_loop(0, 16, send_stage, 0)
 
     eye = lax.broadcasted_iota(jnp.int32, (128, 128), 0) == lax.broadcasted_iota(jnp.int32, (128, 128), 1)
 
@@ -228,9 +249,6 @@
             kself[pl.ds(pl.multiple_of(i * 128, 128), 128), :] = rotate(rx[j, 1, pl.ds(i * 4, 4)].reshape(128, HS), half, i * 128, 128)
             return 0
         lax.fori_loop(0, 4, body, 0)
-
-    def far_chunk(k):
-        return (k + y // 2 + 2) % 4
 
     def serve_partner():
         there = slots(other)
@@ -242,7 +260,7 @@
             top, total, acc = attend(q, [(cache[other, 0, sl], cache[other, 1, sl], b) for sl, b in there])
             oc_out[i] = (acc / total).astype(jnp.bfloat16)
             lse = jnp.broadcast_to(top + jnp.log2(total), (128, 128))
-            lse_out[i] = jnp.broadcast_to(jnp.sum(jnp.where(eye, lse, 0.0), axis=0, keepdims=True), (8, 128))
+            lse_out[i] = jnp.sum(jnp.where(eye, lse, 0.0), axis=0, keepdims=True)
             pltpu.make_async_remote_copy(oc_out.at[i], oc.at[i], s_oc.at[0], r_oc.at[i], device_id=(g, partner), device_id_type=MESH).start()
             pltpu.make_async_remote_copy(lse_out.at[i], lse_in.at[i], s_oc.at[1], r_lse.at[i], device_id=(g, partner), device_id_type=MESH).start()
             return 0
@@ -302,7 +320,7 @@
         top, total, acc = attend(q, [(kself[...], rx[1, 2].reshape(VT, HS), None)])
         pltpu.make_async_copy(lse_in.at[i], lse_in.at[i], r_lse.at[i]).wait()
         pltpu.make_async_copy(oc.at[i], oc.at[i], r_oc.at[i]).wait()
-        lse = jnp.broadcast_to(lse_in[i, 0:1, :], (128, 128))
+        lse = jnp.broadcast_to(lse_in[i], (128, 128))
         lse = jnp.sum(jnp.where(eye, lse, 0.0), axis=1, keepdims=True)
         both = jnp.maximum(lse, top)
         wc = jnp.exp2(lse - both)
@@ -404,8 +422,8 @@
             vmem((HALF, TOK, HS), bf),
             vmem((4, 128, HS), bf),
             vmem((4, 128, HS), bf),
-            vmem((4, 8, 128), f32),
-            vmem((4, 8, 128), f32),
+            vmem((4, 1, 128), f32),
+            vmem((4, 1, 128), f32),
             vmem((2, HALF, TOK, HS), bf),
             vmem((2, 2, CYCLE, VT, HS), bf),
             vmem((3, CH, 2 * CH), bf),

time: 43.4 us -> 42.7 us (0.984)
  Pallas kernels: 42.6 us -> 41.9 us
    pallas_call x1, Pallas kernels: 41.8 us -> 41.1 us  [on_device(): pl.pallas_call(kernel, out_shape=shapes, in_specs=[hbm] * 10, out_specs=(...]
where the time goes in v5:
time: 42.7 us; the launch traced here: 42.6 us
  Pallas kernels  41.9 us (98%)
  between operations  0.64 us (1%)
    pallas_call x1, Pallas kernels, on_device(): pl.pallas_call(kernel, out_shape=shapes, in_specs=[hbm] * 10, out_specs=(...  41.1 us

profile of v5, /device:TPU:1, one launch (start us, length us, event | category | flops | bytes accessed | tf_op | source)
XLA Modules:
  0.0 42.6 jit_solution(5749648767021307192)
XLA Ops:
  0.6 41.1 %rollout.1 = (bf16[32,4096]{1,0:T(8,128)(2,1)S(1)}, bf16[1,6,32,2,384]{4,3,2,1,0:T(2,128)(2,1)S(1)}) custom-call(s32[2]{0:T(128)} %slot_hbm.1, s32[2]{0:T(128)} %count_hbm.1, s32[2]{0:T(128)} %pos_hbm.1, bf16[3,32,4096]{2,1,0:T(8,128)(2,1)} %bitcast.1, bf16[2,2,3,512,128]{4,3,2,1,0:T(8,128)(2,1)} %cache_hbm.1, bf16[2,3,1,32,384]{4,3,2,1,0:T(8,128)(2,1)} %dec_in.1, ...), custom_call_target="tpu_custom_call" | custom-call | tf_op jit(solution)/shard_map/rollout/pallas_call | solution.py:414
  41.8 0.8 %put_out.1 = (bf16[32,4096]{1,0:T(8,128)(2,1)}, bf16[1,6,32,2,384]{4,3,2,1,0:T(2,128)(2,1)}) custom-call(bf16[32,4096]{1,0:T(8,128)(2,1)S(1)} %get-tuple-element.4.a, bf16[1,6,32,2,384]{4,3,2,1,0:T(2,128)(2,1)S(1)} %get-tuple-element.5.b), custom_call_target="tpu_custom_call" | custom-call | tf_op jit(solution)/shard_map/put_out/pallas_call | solution.py:448

commit v6 on v5

--- a/solution.py
+++ b/solution.py
@@ -148,6 +148,27 @@
     for_peers(lambda t: send(0, 3, 0, t, r_a))
     for_peers(lambda t: send(1, 2, 1, t, r_b))
 
+    for cp in ds_copies:
+        cp.wait()
+
+    def send_stage(i, _):
+        gd, sd = (g + i) % 16, (g // 8) * HALF + me
+        src, dst = sendd.at[:, :, :, gd], mid.at[g % 8, :, :, :, half]
+        itself = (gd == g) & (sd == s)
+
+        @pl.when(jnp.logical_not(itself))
+        def _():
+            pltpu.make_async_remote_copy(src, dst, s_dec.at[0], r_mid, device_id=(gd, sd), device_id_type=MESH).start()
+
+        @pl.when(itself)
+        def _():
+            pltpu.make_async_copy(src, dst, r_mid).start()
+        return 0
+
+    @pl.when(half == 1)
+    def _():
+        lax.fori_loop(0, 16, send_stage, 0)
+
     c_tab.wait()
     for cp in c_state:
         cp.wait()
@@ -172,24 +193,7 @@
     def _():
         pl.semaphore_wait(bar, 1)
 
-    for cp in ds_copies:
-        cp.wait()
-
-    def send_stage(i, _):
-        gd, sd = (g + i) % 16, (g // 8) * HALF + me
-        src, dst = sendd.at[:, :, :, gd], mid.at[g % 8, :, :, :, half]
-        itself = (gd == g) & (sd == s)
-
-        @pl.when(jnp.logical_not(itself))
-        def _():
-            pltpu.make_async_remote_copy(src, dst, s_dec.at[0], r_mid, device_id=(gd, sd), device_id_type=MESH).start()
-
-        @pl.when(itself)
-        def _():
-            pltpu.make_async_copy(src, dst, r_mid).start()
-        return 0
-
-    @pl.when((half == 1) | (g // 8 == 0))
+    @pl.when((half == 0) & (g // 8 == 0))
     def _():
         lax.fori_loop(0, 16, send_stage, 0)
 

time: 42.7 us -> 42.4 us (level)
  no operation moved by 1% of the time
where the time goes in v6:
time: 42.4 us; the launch traced here: 42.3 us
  Pallas kernels  41.6 us (98%)
  between operations  0.64 us (2%)
    pallas_call x1, Pallas kernels, on_device(): pl.pallas_call(kernel, out_shape=shapes, in_specs=[hbm] * 10, out_specs=(...  40.8 us

profile of v6, /device:TPU:1, one launch (start us, length us, event | category | flops | bytes accessed | tf_op | source)
XLA Modules:
  0.0 42.3 jit_solution(15450290597878712196)
XLA Ops:
  0.6 40.8 %rollout.1 = (bf16[32,4096]{1,0:T(8,128)(2,1)S(1)}, bf16[1,6,32,2,384]{4,3,2,1,0:T(2,128)(2,1)S(1)}) custom-call(s32[2]{0:T(128)} %slot_hbm.1, s32[2]{0:T(128)} %count_hbm.1, s32[2]{0:T(128)} %pos_hbm.1, bf16[3,32,4096]{2,1,0:T(8,128)(2,1)} %bitcast.1, bf16[2,2,3,512,128]{4,3,2,1,0:T(8,128)(2,1)} %cache_hbm.1, bf16[2,3,1,32,384]{4,3,2,1,0:T(8,128)(2,1)} %dec_in.1, ...), custom_call_target="tpu_custom_call" | custom-call | tf_op jit(solution)/shard_map/rollout/pallas_call | solution.py:418
  41.4 0.8 %put_out.1 = (bf16[32,4096]{1,0:T(8,128)(2,1)}, bf16[1,6,32,2,384]{4,3,2,1,0:T(2,128)(2,1)}) custom-call(bf16[32,4096]{1,0:T(8,128)(2,1)S(1)} %get-tuple-element.4.a, bf16[1,6,32,2,384]{4,3,2,1,0:T(2,128)(2,1)S(1)} %get-tuple-element.5.b), custom_call_target="tpu_custom_call" | custom-call | tf_op jit(solution)/shard_map/put_out/pallas_call | solution.py:452
